TPU v7x, 512 devices: a whole 4x8x8 slice. The times are simulated.
512 devices in a mesh: panel: 32 (over x_hi, y, core), row: 16 (over z, x_lo).
Axes of the slice: x: 4 (x_hi: 2, x_lo: 2; x = x_hi * 2 + x_lo), y: 8, z: 8, core: 2. Of those that a mesh axis runs over, the one named last changes fastest.
Arguments:
- slab: float32 [16384, 8192], P('row', 'panel'), may hold values from -6 to 6
- boundary: float32 [16384, 256], P('row'), may hold values from -6 to 6
- diag_inverse: float32 [8192, 256], P(('panel', 'row')), may hold values from -1 to 1.6, as said below
- sub_block: float32 [8192, 256], P(('panel', 'row')), may hold values from -0.375 to 0.375
- tail_coupling: float32 [8192, 256], P(('panel', 'row')), may hold values from -0.0625 to 0.0625
- tail_cols: float32 [16384, 256], P(('row', 'panel')), may hold values from -6 to 6
Outputs:
- factor: float32 [16384, 8192], P('row', 'panel')
- tail_out: float32 [16384, 256], P(('row', 'panel'))
Inputs may be any that keep to these rules, and one draw needn't show every extreme that they name: `diag_inverse`: each block of 256 rows is lower triangular with a positive diagonal of 0.6 to 1.6.
All inputs are finite; a program needn't handle non-finite values.
Results may differ from a plain program's by a relative error of at most 0.00029.
Values sent between devices are 32-bit elements; how exact they have to be, the bound alone decides.
A program may use at most 128 MiB of HBM per device.

v0:
```python
import jax
import jax.numpy as jnp
from jax import lax
from jax.sharding import PartitionSpec as P

NBATCH = 8


def from_behind(array, axis, by):
    count = lax.axis_size(axis)
    pairs = [(i, i + by) for i in range(count) if 0 <= i + by < count]
    return lax.ppermute(array, axis, pairs)


def transpose_dot(left, right):
    return lax.dot_general(
        left,
        right,
        (((1,), (1,)), ((), ())),
        precision=lax.Precision.HIGHEST,
        preferred_element_type=jnp.float32,
    )


def plain_dot(left, right):
    return jnp.dot(left, right, precision=lax.Precision.HIGHEST, preferred_element_type=jnp.float32)


def on_device(slab, boundary, diag_inverse, sub_block, tail_coupling, tail_cols):
    inverse, beneath, coupling = (
        lax.all_gather(diag_inverse, "row", axis=0, tiled=True),
        lax.all_gather(sub_block, "row", axis=0, tiled=True),
        lax.all_gather(tail_coupling, "row", axis=0, tiled=True),
    )
    is_first = lax.axis_index("panel") == 0
    panels = lax.axis_size("panel")
    batch_rows = slab.shape[0] // NBATCH

    def relay_turn(turn_index, carry_state):
        factor, sent = carry_state
        arrived = from_behind(sent, "panel", 1)
        batch_index = turn_index - lax.axis_index("panel")
        in_range = (batch_index >= 0) & (batch_index < NBATCH)
        offset = jnp.clip(batch_index, 0, NBATCH - 1) * batch_rows
        slab_block = lax.dynamic_slice_in_dim(slab, offset, batch_rows, 0)
        boundary_block = lax.dynamic_slice_in_dim(boundary, offset, batch_rows, 0)
        previous = jnp.where(is_first, boundary_block, arrived)
        solved = transpose_dot(slab_block - transpose_dot(previous, beneath), inverse)
        kept_block = lax.dynamic_slice_in_dim(factor, offset, batch_rows, 0)
        factor = lax.dynamic_update_slice_in_dim(
            factor, jnp.where(in_range, solved, kept_block), offset, 0
        )
        return (factor, solved)

    def pair_turns(loop_index, carry_state):
        return relay_turn(2 * loop_index + 1, relay_turn(2 * loop_index, carry_state))

    start_state = (jnp.zeros_like(slab), jnp.zeros((batch_rows, slab.shape[1]), jnp.float32))
    factor, last_sent = lax.fori_loop(0, (NBATCH + panels) // 2, pair_turns, start_state)
    summed = lax.psum_scatter(plain_dot(factor, coupling), "panel", scatter_dimension=0, tiled=True)
    return (factor, tail_cols - summed)


def solution(mesh):
    placed = (
        P("row", "panel"),
        P("row", None),
        P(("panel", "row"), None),
        P(("panel", "row"), None),
        P(("panel", "row"), None),
        P(("row", "panel"), None),
    )
    return jax.shard_map(
        on_device,
        mesh=mesh,
        in_specs=placed,
        out_specs=(P("row", "panel"), P(("row", "panel"), None)),
        check_vma=False,
    )
```

profile of v0, /device:TPU:57, one launch (start us, length us, event | category | flops | bytes accessed | tf_op | source)
XLA Modules:
  0.0 698.7 jit_solution(6919103032246248816)
XLA Ops:
  7.2 34.3 %all_gather.10 = f32[256,256]{1,0:T(8,128)S(1)} all-gather(f32[16,256]{1,0:T(8,128)} %param.10), channel_id=1, replica_groups=mesh['panel'=32,'row'=16] {'row'}, dimensions={0}, use_global_device_ids=true | all-gather | bytes 278528 | tf_op jit(solution)/shard_map/all_gather | solution.py:31
  41.5 24.1 %all_gather.9 = f32[256,256]{1,0:T(8,128)S(1)} all-gather(f32[16,256]{1,0:T(8,128)S(1)} %copy-done.2), channel_id=1, replica_groups=mesh['panel'=32,'row'=16] {'row'}, dimensions={0}, use_global_device_ids=true | all-gather | bytes 278528 | tf_op jit(solution)/shard_map/all_gather | solution.py:32
  65.6 26.4 %all_gather.11 = f32[256,256]{1,0:T(8,128)S(1)} all-gather(f32[16,256]{1,0:T(8,128)S(1)} %copy-done.3), channel_id=1, replica_groups=mesh['panel'=32,'row'=16] {'row'}, dimensions={0}, use_global_device_ids=true | all-gather | bytes 278528 | tf_op jit(solution)/shard_map/all_gather | solution.py:33
  92.2 484.4 %while.15 = (s32[]{:T(128)}, f32[1024,256]{1,0:T(8,128)S(1)}, f32[128,256]{1,0:T(8,128)S(1)}, f32[1024,256]{1,0:T(8,128)}, pred[]{:T(512)}, /*index=5*/f32[1024,...) while((s32[]{:T(128)}, f32[1024,256]{1,0:T(8,128)S(1)}, ...), condition=%wide.region_1.2_spmd, body=%wide.region_0.1_spmd.sunk | while | flops 402849792 | bytes 4197885 | solution.py:59
  92.2 24.5 %collective-permute-start = (f32[128,256]{1,0:T(8,128)S(1)}, f32[128,256]{1,0:T(8,128)S(1)}, u32[]{:S(2)}, u32[]{:S(2)}) collective-permute-start(f32[128,256]{1,0:T(8,128)S(1)} %get-tuple-element.238), channel_id=1, source_target_pairs={{0,16},{16,32},{32,48},{48,64},{64,80},{80,96},{96,112},{112,128},... | collective-permute-start | bytes 393224 | tf_op jit(solution)/shard_map/while/body/eval_jaxpr/ppermute | solution.py:12
  120.4 8.0 %collective-permute-start.1 = (f32[128,256]{1,0:T(8,128)S(1)}, f32[128,256]{1,0:T(8,128)S(1)}, u32[]{:S(2)}, u32[]{:S(2)}) collective-permute-start(f32[128,256]{1,0:T(8,128)S(1)} %get-tuple-element.216), channel_id=1, source_target_pairs={{0,16},{16,32},{32,48},{48,64},{64,80},{80,96},{96,112},{112,128},... | collective-permute-start | bytes 393224 | tf_op jit(solution)/shard_map/while/body/eval_jaxpr/ppermute | solution.py:12
  128.4 1.9 collective-permute-done.1
  132.1 8.0 %collective-permute-start = (f32[128,256]{1,0:T(8,128)S(1)}, f32[128,256]{1,0:T(8,128)S(1)}, u32[]{:S(2)}, u32[]{:S(2)}) collective-permute-start(f32[128,256]{1,0:T(8,128)S(1)} %get-tuple-element.238), channel_id=1, source_target_pairs={{0,16},{16,32},{32,48},{48,64},{64,80},{80,96},{96,112},{112,128},... | collective-permute-start | bytes 393224 | tf_op jit(solution)/shard_map/while/body/eval_jaxpr/ppermute | solution.py:12
  143.8 8.0 %collective-permute-start.1 = (f32[128,256]{1,0:T(8,128)S(1)}, f32[128,256]{1,0:T(8,128)S(1)}, u32[]{:S(2)}, u32[]{:S(2)}) collective-permute-start(f32[128,256]{1,0:T(8,128)S(1)} %get-tuple-element.216), channel_id=1, source_target_pairs={{0,16},{16,32},{32,48},{48,64},{64,80},{80,96},{96,112},{112,128},... | collective-permute-start | bytes 393224 | tf_op jit(solution)/shard_map/while/body/eval_jaxpr/ppermute | solution.py:12
  151.8 1.9 collective-permute-done.1
  155.5 8.0 %collective-permute-start = (f32[128,256]{1,0:T(8,128)S(1)}, f32[128,256]{1,0:T(8,128)S(1)}, u32[]{:S(2)}, u32[]{:S(2)}) collective-permute-start(f32[128,256]{1,0:T(8,128)S(1)} %get-tuple-element.238), channel_id=1, source_target_pairs={{0,16},{16,32},{32,48},{48,64},{64,80},{80,96},{96,112},{112,128},... | collective-permute-start | bytes 393224 | tf_op jit(solution)/shard_map/while/body/eval_jaxpr/ppermute | solution.py:12
  167.2 8.0 %collective-permute-start.1 = (f32[128,256]{1,0:T(8,128)S(1)}, f32[128,256]{1,0:T(8,128)S(1)}, u32[]{:S(2)}, u32[]{:S(2)}) collective-permute-start(f32[128,256]{1,0:T(8,128)S(1)} %get-tuple-element.216), channel_id=1, source_target_pairs={{0,16},{16,32},{32,48},{48,64},{64,80},{80,96},{96,112},{112,128},... | collective-permute-start | bytes 393224 | tf_op jit(solution)/shard_map/while/body/eval_jaxpr/ppermute | solution.py:12
  175.2 1.9 collective-permute-done.1
  178.9 8.0 %collective-permute-start = (f32[128,256]{1,0:T(8,128)S(1)}, f32[128,256]{1,0:T(8,128)S(1)}, u32[]{:S(2)}, u32[]{:S(2)}) collective-permute-start(f32[128,256]{1,0:T(8,128)S(1)} %get-tuple-element.238), channel_id=1, source_target_pairs={{0,16},{16,32},{32,48},{48,64},{64,80},{80,96},{96,112},{112,128},... | collective-permute-start | bytes 393224 | tf_op jit(solution)/shard_map/while/body/eval_jaxpr/ppermute | solution.py:12
  190.6 8.0 %collective-permute-start.1 = (f32[128,256]{1,0:T(8,128)S(1)}, f32[128,256]{1,0:T(8,128)S(1)}, u32[]{:S(2)}, u32[]{:S(2)}) collective-permute-start(f32[128,256]{1,0:T(8,128)S(1)} %get-tuple-element.216), channel_id=1, source_target_pairs={{0,16},{16,32},{32,48},{48,64},{64,80},{80,96},{96,112},{112,128},... | collective-permute-start | bytes 393224 | tf_op jit(solution)/shard_map/while/body/eval_jaxpr/ppermute | solution.py:12
  198.6 1.9 collective-permute-done.1
  202.3 8.0 %collective-permute-start = (f32[128,256]{1,0:T(8,128)S(1)}, f32[128,256]{1,0:T(8,128)S(1)}, u32[]{:S(2)}, u32[]{:S(2)}) collective-permute-start(f32[128,256]{1,0:T(8,128)S(1)} %get-tuple-element.238), channel_id=1, source_target_pairs={{0,16},{16,32},{32,48},{48,64},{64,80},{80,96},{96,112},{112,128},... | collective-permute-start | bytes 393224 | tf_op jit(solution)/shard_map/while/body/eval_jaxpr/ppermute | solution.py:12
  214.0 8.0 %collective-permute-start.1 = (f32[128,256]{1,0:T(8,128)S(1)}, f32[128,256]{1,0:T(8,128)S(1)}, u32[]{:S(2)}, u32[]{:S(2)}) collective-permute-start(f32[128,256]{1,0:T(8,128)S(1)} %get-tuple-element.216), channel_id=1, source_target_pairs={{0,16},{16,32},{32,48},{48,64},{64,80},{80,96},{96,112},{112,128},... | collective-permute-start | bytes 393224 | tf_op jit(solution)/shard_map/while/body/eval_jaxpr/ppermute | solution.py:12
  222.0 1.9 collective-permute-done.1
  225.7 8.0 %collective-permute-start = (f32[128,256]{1,0:T(8,128)S(1)}, f32[128,256]{1,0:T(8,128)S(1)}, u32[]{:S(2)}, u32[]{:S(2)}) collective-permute-start(f32[128,256]{1,0:T(8,128)S(1)} %get-tuple-element.238), channel_id=1, source_target_pairs={{0,16},{16,32},{32,48},{48,64},{64,80},{80,96},{96,112},{112,128},... | collective-permute-start | bytes 393224 | tf_op jit(solution)/shard_map/while/body/eval_jaxpr/ppermute | solution.py:12
  237.4 8.0 %collective-permute-start.1 = (f32[128,256]{1,0:T(8,128)S(1)}, f32[128,256]{1,0:T(8,128)S(1)}, u32[]{:S(2)}, u32[]{:S(2)}) collective-permute-start(f32[128,256]{1,0:T(8,128)S(1)} %get-tuple-element.216), channel_id=1, source_target_pairs={{0,16},{16,32},{32,48},{48,64},{64,80},{80,96},{96,112},{112,128},... | collective-permute-start | bytes 393224 | tf_op jit(solution)/shard_map/while/body/eval_jaxpr/ppermute | solution.py:12
  245.4 1.9 collective-permute-done.1
  249.1 8.0 %collective-permute-start = (f32[128,256]{1,0:T(8,128)S(1)}, f32[128,256]{1,0:T(8,128)S(1)}, u32[]{:S(2)}, u32[]{:S(2)}) collective-permute-start(f32[128,256]{1,0:T(8,128)S(1)} %get-tuple-element.238), channel_id=1, source_target_pairs={{0,16},{16,32},{32,48},{48,64},{64,80},{80,96},{96,112},{112,128},... | collective-permute-start | bytes 393224 | tf_op jit(solution)/shard_map/while/body/eval_jaxpr/ppermute | solution.py:12
  260.8 8.0 %collective-permute-start.1 = (f32[128,256]{1,0:T(8,128)S(1)}, f32[128,256]{1,0:T(8,128)S(1)}, u32[]{:S(2)}, u32[]{:S(2)}) collective-permute-start(f32[128,256]{1,0:T(8,128)S(1)} %get-tuple-element.216), channel_id=1, source_target_pairs={{0,16},{16,32},{32,48},{48,64},{64,80},{80,96},{96,112},{112,128},... | collective-permute-start | bytes 393224 | tf_op jit(solution)/shard_map/while/body/eval_jaxpr/ppermute | solution.py:12
  268.8 1.9 collective-permute-done.1
  272.5 8.0 %collective-permute-start = (f32[128,256]{1,0:T(8,128)S(1)}, f32[128,256]{1,0:T(8,128)S(1)}, u32[]{:S(2)}, u32[]{:S(2)}) collective-permute-start(f32[128,256]{1,0:T(8,128)S(1)} %get-tuple-element.238), channel_id=1, source_target_pairs={{0,16},{16,32},{32,48},{48,64},{64,80},{80,96},{96,112},{112,128},... | collective-permute-start | bytes 393224 | tf_op jit(solution)/shard_map/while/body/eval_jaxpr/ppermute | solution.py:12
  284.2 8.0 %collective-permute-start.1 = (f32[128,256]{1,0:T(8,128)S(1)}, f32[128,256]{1,0:T(8,128)S(1)}, u32[]{:S(2)}, u32[]{:S(2)}) collective-permute-start(f32[128,256]{1,0:T(8,128)S(1)} %get-tuple-element.216), channel_id=1, source_target_pairs={{0,16},{16,32},{32,48},{48,64},{64,80},{80,96},{96,112},{112,128},... | collective-permute-start | bytes 393224 | tf_op jit(solution)/shard_map/while/body/eval_jaxpr/ppermute | solution.py:12
  292.2 1.9 collective-permute-done.1
  295.9 8.0 %collective-permute-start = (f32[128,256]{1,0:T(8,128)S(1)}, f32[128,256]{1,0:T(8,128)S(1)}, u32[]{:S(2)}, u32[]{:S(2)}) collective-permute-start(f32[128,256]{1,0:T(8,128)S(1)} %get-tuple-element.238), channel_id=1, source_target_pairs={{0,16},{16,32},{32,48},{48,64},{64,80},{80,96},{96,112},{112,128},... | collective-permute-start | bytes 393224 | tf_op jit(solution)/shard_map/while/body/eval_jaxpr/ppermute | solution.py:12
  307.6 8.0 %collective-permute-start.1 = (f32[128,256]{1,0:T(8,128)S(1)}, f32[128,256]{1,0:T(8,128)S(1)}, u32[]{:S(2)}, u32[]{:S(2)}) collective-permute-start(f32[128,256]{1,0:T(8,128)S(1)} %get-tuple-element.216), channel_id=1, source_target_pairs={{0,16},{16,32},{32,48},{48,64},{64,80},{80,96},{96,112},{112,128},... | collective-permute-start | bytes 393224 | tf_op jit(solution)/shard_map/while/body/eval_jaxpr/ppermute | solution.py:12
  315.6 1.9 collective-permute-done.1
  319.3 8.0 %collective-permute-start = (f32[128,256]{1,0:T(8,128)S(1)}, f32[128,256]{1,0:T(8,128)S(1)}, u32[]{:S(2)}, u32[]{:S(2)}) collective-permute-start(f32[128,256]{1,0:T(8,128)S(1)} %get-tuple-element.238), channel_id=1, source_target_pairs={{0,16},{16,32},{32,48},{48,64},{64,80},{80,96},{96,112},{112,128},... | collective-permute-start | bytes 393224 | tf_op jit(solution)/shard_map/while/body/eval_jaxpr/ppermute | solution.py:12
  331.0 8.0 %collective-permute-start.1 = (f32[128,256]{1,0:T(8,128)S(1)}, f32[128,256]{1,0:T(8,128)S(1)}, u32[]{:S(2)}, u32[]{:S(2)}) collective-permute-start(f32[128,256]{1,0:T(8,128)S(1)} %get-tuple-element.216), channel_id=1, source_target_pairs={{0,16},{16,32},{32,48},{48,64},{64,80},{80,96},{96,112},{112,128},... | collective-permute-start | bytes 393224 | tf_op jit(solution)/shard_map/while/body/eval_jaxpr/ppermute | solution.py:12
  339.0 1.9 collective-permute-done.1
  342.7 8.0 %collective-permute-start = (f32[128,256]{1,0:T(8,128)S(1)}, f32[128,256]{1,0:T(8,128)S(1)}, u32[]{:S(2)}, u32[]{:S(2)}) collective-permute-start(f32[128,256]{1,0:T(8,128)S(1)} %get-tuple-element.238), channel_id=1, source_target_pairs={{0,16},{16,32},{32,48},{48,64},{64,80},{80,96},{96,112},{112,128},... | collective-permute-start | bytes 393224 | tf_op jit(solution)/shard_map/while/body/eval_jaxpr/ppermute | solution.py:12
  354.3 8.0 %collective-permute-start.1 = (f32[128,256]{1,0:T(8,128)S(1)}, f32[128,256]{1,0:T(8,128)S(1)}, u32[]{:S(2)}, u32[]{:S(2)}) collective-permute-start(f32[128,256]{1,0:T(8,128)S(1)} %get-tuple-element.216), channel_id=1, source_target_pairs={{0,16},{16,32},{32,48},{48,64},{64,80},{80,96},{96,112},{112,128},... | collective-permute-start | bytes 393224 | tf_op jit(solution)/shard_map/while/body/eval_jaxpr/ppermute | solution.py:12
  362.3 1.9 collective-permute-done.1
  366.1 8.0 %collective-permute-start = (f32[128,256]{1,0:T(8,128)S(1)}, f32[128,256]{1,0:T(8,128)S(1)}, u32[]{:S(2)}, u32[]{:S(2)}) collective-permute-start(f32[128,256]{1,0:T(8,128)S(1)} %get-tuple-element.238), channel_id=1, source_target_pairs={{0,16},{16,32},{32,48},{48,64},{64,80},{80,96},{96,112},{112,128},... | collective-permute-start | bytes 393224 | tf_op jit(solution)/shard_map/while/body/eval_jaxpr/ppermute | solution.py:12
  377.7 8.0 %collective-permute-start.1 = (f32[128,256]{1,0:T(8,128)S(1)}, f32[128,256]{1,0:T(8,128)S(1)}, u32[]{:S(2)}, u32[]{:S(2)}) collective-permute-start(f32[128,256]{1,0:T(8,128)S(1)} %get-tuple-element.216), channel_id=1, source_target_pairs={{0,16},{16,32},{32,48},{48,64},{64,80},{80,96},{96,112},{112,128},... | collective-permute-start | bytes 393224 | tf_op jit(solution)/shard_map/while/body/eval_jaxpr/ppermute | solution.py:12
  385.7 1.9 collective-permute-done.1
  389.4 8.0 %collective-permute-start = (f32[128,256]{1,0:T(8,128)S(1)}, f32[128,256]{1,0:T(8,128)S(1)}, u32[]{:S(2)}, u32[]{:S(2)}) collective-permute-start(f32[128,256]{1,0:T(8,128)S(1)} %get-tuple-element.238), channel_id=1, source_target_pairs={{0,16},{16,32},{32,48},{48,64},{64,80},{80,96},{96,112},{112,128},... | collective-permute-start | bytes 393224 | tf_op jit(solution)/shard_map/while/body/eval_jaxpr/ppermute | solution.py:12
  401.1 8.0 %collective-permute-start.1 = (f32[128,256]{1,0:T(8,128)S(1)}, f32[128,256]{1,0:T(8,128)S(1)}, u32[]{:S(2)}, u32[]{:S(2)}) collective-permute-start(f32[128,256]{1,0:T(8,128)S(1)} %get-tuple-element.216), channel_id=1, source_target_pairs={{0,16},{16,32},{32,48},{48,64},{64,80},{80,96},{96,112},{112,128},... | collective-permute-start | bytes 393224 | tf_op jit(solution)/shard_map/while/body/eval_jaxpr/ppermute | solution.py:12
  409.1 1.9 collective-permute-done.1
  412.8 8.0 %collective-permute-start = (f32[128,256]{1,0:T(8,128)S(1)}, f32[128,256]{1,0:T(8,128)S(1)}, u32[]{:S(2)}, u32[]{:S(2)}) collective-permute-start(f32[128,256]{1,0:T(8,128)S(1)} %get-tuple-element.238), channel_id=1, source_target_pairs={{0,16},{16,32},{32,48},{48,64},{64,80},{80,96},{96,112},{112,128},... | collective-permute-start | bytes 393224 | tf_op jit(solution)/shard_map/while/body/eval_jaxpr/ppermute | solution.py:12
  424.5 8.0 %collective-permute-start.1 = (f32[128,256]{1,0:T(8,128)S(1)}, f32[128,256]{1,0:T(8,128)S(1)}, u32[]{:S(2)}, u32[]{:S(2)}) collective-permute-start(f32[128,256]{1,0:T(8,128)S(1)} %get-tuple-element.216), channel_id=1, source_target_pairs={{0,16},{16,32},{32,48},{48,64},{64,80},{80,96},{96,112},{112,128},... | collective-permute-start | bytes 393224 | tf_op jit(solution)/shard_map/while/body/eval_jaxpr/ppermute | solution.py:12
  432.5 1.9 collective-permute-done.1
  436.2 8.0 %collective-permute-start = (f32[128,256]{1,0:T(8,128)S(1)}, f32[128,256]{1,0:T(8,128)S(1)}, u32[]{:S(2)}, u32[]{:S(2)}) collective-permute-start(f32[128,256]{1,0:T(8,128)S(1)} %get-tuple-element.238), channel_id=1, source_target_pairs={{0,16},{16,32},{32,48},{48,64},{64,80},{80,96},{96,112},{112,128},... | collective-permute-start | bytes 393224 | tf_op jit(solution)/shard_map/while/body/eval_jaxpr/ppermute | solution.py:12
  447.9 8.0 %collective-permute-start.1 = (f32[128,256]{1,0:T(8,128)S(1)}, f32[128,256]{1,0:T(8,128)S(1)}, u32[]{:S(2)}, u32[]{:S(2)}) collective-permute-start(f32[128,256]{1,0:T(8,128)S(1)} %get-tuple-element.216), channel_id=1, source_target_pairs={{0,16},{16,32},{32,48},{48,64},{64,80},{80,96},{96,112},{112,128},... | collective-permute-start | bytes 393224 | tf_op jit(solution)/shard_map/while/body/eval_jaxpr/ppermute | solution.py:12
  455.9 1.9 collective-permute-done.1
  459.6 8.0 %collective-permute-start = (f32[128,256]{1,0:T(8,128)S(1)}, f32[128,256]{1,0:T(8,128)S(1)}, u32[]{:S(2)}, u32[]{:S(2)}) collective-permute-start(f32[128,256]{1,0:T(8,128)S(1)} %get-tuple-element.238), channel_id=1, source_target_pairs={{0,16},{16,32},{32,48},{48,64},{64,80},{80,96},{96,112},{112,128},... | collective-permute-start | bytes 393224 | tf_op jit(solution)/shard_map/while/body/eval_jaxpr/ppermute | solution.py:12
  471.3 8.0 %collective-permute-start.1 = (f32[128,256]{1,0:T(8,128)S(1)}, f32[128,256]{1,0:T(8,128)S(1)}, u32[]{:S(2)}, u32[]{:S(2)}) collective-permute-start(f32[128,256]{1,0:T(8,128)S(1)} %get-tuple-element.216), channel_id=1, source_target_pairs={{0,16},{16,32},{32,48},{48,64},{64,80},{80,96},{96,112},{112,128},... | collective-permute-start | bytes 393224 | tf_op jit(solution)/shard_map/while/body/eval_jaxpr/ppermute | solution.py:12
  483.0 8.0 %collective-permute-start = (f32[128,256]{1,0:T(8,128)S(1)}, f32[128,256]{1,0:T(8,128)S(1)}, u32[]{:S(2)}, u32[]{:S(2)}) collective-permute-start(f32[128,256]{1,0:T(8,128)S(1)} %get-tuple-element.238), channel_id=1, source_target_pairs={{0,16},{16,32},{32,48},{48,64},{64,80},{80,96},{96,112},{112,128},... | collective-permute-start | bytes 393224 | tf_op jit(solution)/shard_map/while/body/eval_jaxpr/ppermute | solution.py:12
  494.7 8.0 %collective-permute-start.1 = (f32[128,256]{1,0:T(8,128)S(1)}, f32[128,256]{1,0:T(8,128)S(1)}, u32[]{:S(2)}, u32[]{:S(2)}) collective-permute-start(f32[128,256]{1,0:T(8,128)S(1)} %get-tuple-element.216), channel_id=1, source_target_pairs={{0,16},{16,32},{32,48},{48,64},{64,80},{80,96},{96,112},{112,128},... | collective-permute-start | bytes 393224 | tf_op jit(solution)/shard_map/while/body/eval_jaxpr/ppermute | solution.py:12
  502.7 1.9 collective-permute-done.1
  506.4 8.0 %collective-permute-start = (f32[128,256]{1,0:T(8,128)S(1)}, f32[128,256]{1,0:T(8,128)S(1)}, u32[]{:S(2)}, u32[]{:S(2)}) collective-permute-start(f32[128,256]{1,0:T(8,128)S(1)} %get-tuple-element.238), channel_id=1, source_target_pairs={{0,16},{16,32},{32,48},{48,64},{64,80},{80,96},{96,112},{112,128},... | collective-permute-start | bytes 393224 | tf_op jit(solution)/shard_map/while/body/eval_jaxpr/ppermute | solution.py:12
  518.1 8.0 %collective-permute-start.1 = (f32[128,256]{1,0:T(8,128)S(1)}, f32[128,256]{1,0:T(8,128)S(1)}, u32[]{:S(2)}, u32[]{:S(2)}) collective-permute-start(f32[128,256]{1,0:T(8,128)S(1)} %get-tuple-element.216), channel_id=1, source_target_pairs={{0,16},{16,32},{32,48},{48,64},{64,80},{80,96},{96,112},{112,128},... | collective-permute-start | bytes 393224 | tf_op jit(solution)/shard_map/while/body/eval_jaxpr/ppermute | solution.py:12
  526.1 1.9 collective-permute-done.1
  529.8 8.0 %collective-permute-start = (f32[128,256]{1,0:T(8,128)S(1)}, f32[128,256]{1,0:T(8,128)S(1)}, u32[]{:S(2)}, u32[]{:S(2)}) collective-permute-start(f32[128,256]{1,0:T(8,128)S(1)} %get-tuple-element.238), channel_id=1, source_target_pairs={{0,16},{16,32},{32,48},{48,64},{64,80},{80,96},{96,112},{112,128},... | collective-permute-start | bytes 393224 | tf_op jit(solution)/shard_map/while/body/eval_jaxpr/ppermute | solution.py:12
  541.5 8.0 %collective-permute-start.1 = (f32[128,256]{1,0:T(8,128)S(1)}, f32[128,256]{1,0:T(8,128)S(1)}, u32[]{:S(2)}, u32[]{:S(2)}) collective-permute-start(f32[128,256]{1,0:T(8,128)S(1)} %get-tuple-element.216), channel_id=1, source_target_pairs={{0,16},{16,32},{32,48},{48,64},{64,80},{80,96},{96,112},{112,128},... | collective-permute-start | bytes 393224 | tf_op jit(solution)/shard_map/while/body/eval_jaxpr/ppermute | solution.py:12
  549.5 1.9 collective-permute-done.1
  553.2 8.0 %collective-permute-start = (f32[128,256]{1,0:T(8,128)S(1)}, f32[128,256]{1,0:T(8,128)S(1)}, u32[]{:S(2)}, u32[]{:S(2)}) collective-permute-start(f32[128,256]{1,0:T(8,128)S(1)} %get-tuple-element.238), channel_id=1, source_target_pairs={{0,16},{16,32},{32,48},{48,64},{64,80},{80,96},{96,112},{112,128},... | collective-permute-start | bytes 393224 | tf_op jit(solution)/shard_map/while/body/eval_jaxpr/ppermute | solution.py:12
  564.9 8.0 %collective-permute-start.1 = (f32[128,256]{1,0:T(8,128)S(1)}, f32[128,256]{1,0:T(8,128)S(1)}, u32[]{:S(2)}, u32[]{:S(2)}) collective-permute-start(f32[128,256]{1,0:T(8,128)S(1)} %get-tuple-element.216), channel_id=1, source_target_pairs={{0,16},{16,32},{32,48},{48,64},{64,80},{80,96},{96,112},{112,128},... | collective-permute-start | bytes 393224 | tf_op jit(solution)/shard_map/while/body/eval_jaxpr/ppermute | solution.py:12
  576.6 2.0 fusion.8
  578.6 111.8 %reduce-scatter.2.cloned.1.call-done = f32[32,256]{1,0:T(8,128)} async-done(((f32[1024,256]{1,0:T(8,128)}), f32[32,256]{1,0:T(8,128)}) %reduce-scatter.2.cloned.1.call-update) | async-done | bytes 32784 | tf_op jit(solution)/shard_map/reduce_scatter | solution.py:60
  (115 shorter events, 114.3 us)
Async XLA Ops:
  7.2 683.3 %reduce-scatter.2.cloned.1.call-start = ((), (), s32[]{:S(2)}) async-start(), calls=%async_computation.1 | async-start | bytes 1081344 | tf_op jit(solution)/shard_map/reduce_scatter | solution.py:60
  7.2 34.3 %copy-start.2 = (f32[16,256]{1,0:T(8,128)S(1)}, f32[16,256]{1,0:T(8,128)}, u32[]{:S(2)}) copy-start(f32[16,256]{1,0:T(8,128)} %param.11) | copy-start | bytes 49156
  41.5 24.2 %copy-start.3 = (f32[16,256]{1,0:T(8,128)S(1)}, f32[16,256]{1,0:T(8,128)}, u32[]{:S(2)}) copy-start(f32[16,256]{1,0:T(8,128)} %param.12) | copy-start | bytes 49156
  92.2 26.5 %collective-permute-start = (f32[128,256]{1,0:T(8,128)S(1)}, f32[128,256]{1,0:T(8,128)S(1)}, u32[]{:S(2)}, u32[]{:S(2)}) collective-permute-start(f32[128,256]{1,0:T(8,128)S(1)} %get-tuple-element.238), channel_id=1, source_target_pairs={{0,16},{16,32},{32,48},{48,64},{64,80},{80,96},{96,112},{112,128},... | collective-permute-start | bytes 393224 | tf_op jit(solution)/shard_map/while/body/eval_jaxpr/ppermute | solution.py:12
  120.4 9.9 %collective-permute-start.1 = (f32[128,256]{1,0:T(8,128)S(1)}, f32[128,256]{1,0:T(8,128)S(1)}, u32[]{:S(2)}, u32[]{:S(2)}) collective-permute-start(f32[128,256]{1,0:T(8,128)S(1)} %get-tuple-element.216), channel_id=1, source_target_pairs={{0,16},{16,32},{32,48},{48,64},{64,80},{80,96},{96,112},{112,128},... | collective-permute-start | bytes 393224 | tf_op jit(solution)/shard_map/while/body/eval_jaxpr/ppermute | solution.py:12
  132.1 9.9 %collective-permute-start = (f32[128,256]{1,0:T(8,128)S(1)}, f32[128,256]{1,0:T(8,128)S(1)}, u32[]{:S(2)}, u32[]{:S(2)}) collective-permute-start(f32[128,256]{1,0:T(8,128)S(1)} %get-tuple-element.238), channel_id=1, source_target_pairs={{0,16},{16,32},{32,48},{48,64},{64,80},{80,96},{96,112},{112,128},... | collective-permute-start | bytes 393224 | tf_op jit(solution)/shard_map/while/body/eval_jaxpr/ppermute | solution.py:12
  143.8 9.9 %collective-permute-start.1 = (f32[128,256]{1,0:T(8,128)S(1)}, f32[128,256]{1,0:T(8,128)S(1)}, u32[]{:S(2)}, u32[]{:S(2)}) collective-permute-start(f32[128,256]{1,0:T(8,128)S(1)} %get-tuple-element.216), channel_id=1, source_target_pairs={{0,16},{16,32},{32,48},{48,64},{64,80},{80,96},{96,112},{112,128},... | collective-permute-start | bytes 393224 | tf_op jit(solution)/shard_map/while/body/eval_jaxpr/ppermute | solution.py:12
  155.5 9.9 %collective-permute-start = (f32[128,256]{1,0:T(8,128)S(1)}, f32[128,256]{1,0:T(8,128)S(1)}, u32[]{:S(2)}, u32[]{:S(2)}) collective-permute-start(f32[128,256]{1,0:T(8,128)S(1)} %get-tuple-element.238), channel_id=1, source_target_pairs={{0,16},{16,32},{32,48},{48,64},{64,80},{80,96},{96,112},{112,128},... | collective-permute-start | bytes 393224 | tf_op jit(solution)/shard_map/while/body/eval_jaxpr/ppermute | solution.py:12
  167.2 9.9 %collective-permute-start.1 = (f32[128,256]{1,0:T(8,128)S(1)}, f32[128,256]{1,0:T(8,128)S(1)}, u32[]{:S(2)}, u32[]{:S(2)}) collective-permute-start(f32[128,256]{1,0:T(8,128)S(1)} %get-tuple-element.216), channel_id=1, source_target_pairs={{0,16},{16,32},{32,48},{48,64},{64,80},{80,96},{96,112},{112,128},... | collective-permute-start | bytes 393224 | tf_op jit(solution)/shard_map/while/body/eval_jaxpr/ppermute | solution.py:12
  178.9 9.9 %collective-permute-start = (f32[128,256]{1,0:T(8,128)S(1)}, f32[128,256]{1,0:T(8,128)S(1)}, u32[]{:S(2)}, u32[]{:S(2)}) collective-permute-start(f32[128,256]{1,0:T(8,128)S(1)} %get-tuple-element.238), channel_id=1, source_target_pairs={{0,16},{16,32},{32,48},{48,64},{64,80},{80,96},{96,112},{112,128},... | collective-permute-start | bytes 393224 | tf_op jit(solution)/shard_map/while/body/eval_jaxpr/ppermute | solution.py:12
  190.6 9.9 %collective-permute-start.1 = (f32[128,256]{1,0:T(8,128)S(1)}, f32[128,256]{1,0:T(8,128)S(1)}, u32[]{:S(2)}, u32[]{:S(2)}) collective-permute-start(f32[128,256]{1,0:T(8,128)S(1)} %get-tuple-element.216), channel_id=1, source_target_pairs={{0,16},{16,32},{32,48},{48,64},{64,80},{80,96},{96,112},{112,128},... | collective-permute-start | bytes 393224 | tf_op jit(solution)/shard_map/while/body/eval_jaxpr/ppermute | solution.py:12
  202.3 9.9 %collective-permute-start = (f32[128,256]{1,0:T(8,128)S(1)}, f32[128,256]{1,0:T(8,128)S(1)}, u32[]{:S(2)}, u32[]{:S(2)}) collective-permute-start(f32[128,256]{1,0:T(8,128)S(1)} %get-tuple-element.238), channel_id=1, source_target_pairs={{0,16},{16,32},{32,48},{48,64},{64,80},{80,96},{96,112},{112,128},... | collective-permute-start | bytes 393224 | tf_op jit(solution)/shard_map/while/body/eval_jaxpr/ppermute | solution.py:12
  214.0 9.9 %collective-permute-start.1 = (f32[128,256]{1,0:T(8,128)S(1)}, f32[128,256]{1,0:T(8,128)S(1)}, u32[]{:S(2)}, u32[]{:S(2)}) collective-permute-start(f32[128,256]{1,0:T(8,128)S(1)} %get-tuple-element.216), channel_id=1, source_target_pairs={{0,16},{16,32},{32,48},{48,64},{64,80},{80,96},{96,112},{112,128},... | collective-permute-start | bytes 393224 | tf_op jit(solution)/shard_map/while/body/eval_jaxpr/ppermute | solution.py:12
  225.7 9.9 %collective-permute-start = (f32[128,256]{1,0:T(8,128)S(1)}, f32[128,256]{1,0:T(8,128)S(1)}, u32[]{:S(2)}, u32[]{:S(2)}) collective-permute-start(f32[128,256]{1,0:T(8,128)S(1)} %get-tuple-element.238), channel_id=1, source_target_pairs={{0,16},{16,32},{32,48},{48,64},{64,80},{80,96},{96,112},{112,128},... | collective-permute-start | bytes 393224 | tf_op jit(solution)/shard_map/while/body/eval_jaxpr/ppermute | solution.py:12
  237.4 9.9 %collective-permute-start.1 = (f32[128,256]{1,0:T(8,128)S(1)}, f32[128,256]{1,0:T(8,128)S(1)}, u32[]{:S(2)}, u32[]{:S(2)}) collective-permute-start(f32[128,256]{1,0:T(8,128)S(1)} %get-tuple-element.216), channel_id=1, source_target_pairs={{0,16},{16,32},{32,48},{48,64},{64,80},{80,96},{96,112},{112,128},... | collective-permute-start | bytes 393224 | tf_op jit(solution)/shard_map/while/body/eval_jaxpr/ppermute | solution.py:12
  249.1 9.9 %collective-permute-start = (f32[128,256]{1,0:T(8,128)S(1)}, f32[128,256]{1,0:T(8,128)S(1)}, u32[]{:S(2)}, u32[]{:S(2)}) collective-permute-start(f32[128,256]{1,0:T(8,128)S(1)} %get-tuple-element.238), channel_id=1, source_target_pairs={{0,16},{16,32},{32,48},{48,64},{64,80},{80,96},{96,112},{112,128},... | collective-permute-start | bytes 393224 | tf_op jit(solution)/shard_map/while/body/eval_jaxpr/ppermute | solution.py:12
  260.8 9.9 %collective-permute-start.1 = (f32[128,256]{1,0:T(8,128)S(1)}, f32[128,256]{1,0:T(8,128)S(1)}, u32[]{:S(2)}, u32[]{:S(2)}) collective-permute-start(f32[128,256]{1,0:T(8,128)S(1)} %get-tuple-element.216), channel_id=1, source_target_pairs={{0,16},{16,32},{32,48},{48,64},{64,80},{80,96},{96,112},{112,128},... | collective-permute-start | bytes 393224 | tf_op jit(solution)/shard_map/while/body/eval_jaxpr/ppermute | solution.py:12
  272.5 9.9 %collective-permute-start = (f32[128,256]{1,0:T(8,128)S(1)}, f32[128,256]{1,0:T(8,128)S(1)}, u32[]{:S(2)}, u32[]{:S(2)}) collective-permute-start(f32[128,256]{1,0:T(8,128)S(1)} %get-tuple-element.238), channel_id=1, source_target_pairs={{0,16},{16,32},{32,48},{48,64},{64,80},{80,96},{96,112},{112,128},... | collective-permute-start | bytes 393224 | tf_op jit(solution)/shard_map/while/body/eval_jaxpr/ppermute | solution.py:12
  284.2 9.9 %collective-permute-start.1 = (f32[128,256]{1,0:T(8,128)S(1)}, f32[128,256]{1,0:T(8,128)S(1)}, u32[]{:S(2)}, u32[]{:S(2)}) collective-permute-start(f32[128,256]{1,0:T(8,128)S(1)} %get-tuple-element.216), channel_id=1, source_target_pairs={{0,16},{16,32},{32,48},{48,64},{64,80},{80,96},{96,112},{112,128},... | collective-permute-start | bytes 393224 | tf_op jit(solution)/shard_map/while/body/eval_jaxpr/ppermute | solution.py:12
  295.9 9.9 %collective-permute-start = (f32[128,256]{1,0:T(8,128)S(1)}, f32[128,256]{1,0:T(8,128)S(1)}, u32[]{:S(2)}, u32[]{:S(2)}) collective-permute-start(f32[128,256]{1,0:T(8,128)S(1)} %get-tuple-element.238), channel_id=1, source_target_pairs={{0,16},{16,32},{32,48},{48,64},{64,80},{80,96},{96,112},{112,128},... | collective-permute-start | bytes 393224 | tf_op jit(solution)/shard_map/while/body/eval_jaxpr/ppermute | solution.py:12
  307.6 9.9 %collective-permute-start.1 = (f32[128,256]{1,0:T(8,128)S(1)}, f32[128,256]{1,0:T(8,128)S(1)}, u32[]{:S(2)}, u32[]{:S(2)}) collective-permute-start(f32[128,256]{1,0:T(8,128)S(1)} %get-tuple-element.216), channel_id=1, source_target_pairs={{0,16},{16,32},{32,48},{48,64},{64,80},{80,96},{96,112},{112,128},... | collective-permute-start | bytes 393224 | tf_op jit(solution)/shard_map/while/body/eval_jaxpr/ppermute | solution.py:12
  319.3 9.9 %collective-permute-start = (f32[128,256]{1,0:T(8,128)S(1)}, f32[128,256]{1,0:T(8,128)S(1)}, u32[]{:S(2)}, u32[]{:S(2)}) collective-permute-start(f32[128,256]{1,0:T(8,128)S(1)} %get-tuple-element.238), channel_id=1, source_target_pairs={{0,16},{16,32},{32,48},{48,64},{64,80},{80,96},{96,112},{112,128},... | collective-permute-start | bytes 393224 | tf_op jit(solution)/shard_map/while/body/eval_jaxpr/ppermute | solution.py:12
  331.0 9.9 %collective-permute-start.1 = (f32[128,256]{1,0:T(8,128)S(1)}, f32[128,256]{1,0:T(8,128)S(1)}, u32[]{:S(2)}, u32[]{:S(2)}) collective-permute-start(f32[128,256]{1,0:T(8,128)S(1)} %get-tuple-element.216), channel_id=1, source_target_pairs={{0,16},{16,32},{32,48},{48,64},{64,80},{80,96},{96,112},{112,128},... | collective-permute-start | bytes 393224 | tf_op jit(solution)/shard_map/while/body/eval_jaxpr/ppermute | solution.py:12
  342.7 9.9 %collective-permute-start = (f32[128,256]{1,0:T(8,128)S(1)}, f32[128,256]{1,0:T(8,128)S(1)}, u32[]{:S(2)}, u32[]{:S(2)}) collective-permute-start(f32[128,256]{1,0:T(8,128)S(1)} %get-tuple-element.238), channel_id=1, source_target_pairs={{0,16},{16,32},{32,48},{48,64},{64,80},{80,96},{96,112},{112,128},... | collective-permute-start | bytes 393224 | tf_op jit(solution)/shard_map/while/body/eval_jaxpr/ppermute | solution.py:12
  354.3 9.9 %collective-permute-start.1 = (f32[128,256]{1,0:T(8,128)S(1)}, f32[128,256]{1,0:T(8,128)S(1)}, u32[]{:S(2)}, u32[]{:S(2)}) collective-permute-start(f32[128,256]{1,0:T(8,128)S(1)} %get-tuple-element.216), channel_id=1, source_target_pairs={{0,16},{16,32},{32,48},{48,64},{64,80},{80,96},{96,112},{112,128},... | collective-permute-start | bytes 393224 | tf_op jit(solution)/shard_map/while/body/eval_jaxpr/ppermute | solution.py:12
  366.1 9.9 %collective-permute-start = (f32[128,256]{1,0:T(8,128)S(1)}, f32[128,256]{1,0:T(8,128)S(1)}, u32[]{:S(2)}, u32[]{:S(2)}) collective-permute-start(f32[128,256]{1,0:T(8,128)S(1)} %get-tuple-element.238), channel_id=1, source_target_pairs={{0,16},{16,32},{32,48},{48,64},{64,80},{80,96},{96,112},{112,128},... | collective-permute-start | bytes 393224 | tf_op jit(solution)/shard_map/while/body/eval_jaxpr/ppermute | solution.py:12
  377.7 9.9 %collective-permute-start.1 = (f32[128,256]{1,0:T(8,128)S(1)}, f32[128,256]{1,0:T(8,128)S(1)}, u32[]{:S(2)}, u32[]{:S(2)}) collective-permute-start(f32[128,256]{1,0:T(8,128)S(1)} %get-tuple-element.216), channel_id=1, source_target_pairs={{0,16},{16,32},{32,48},{48,64},{64,80},{80,96},{96,112},{112,128},... | collective-permute-start | bytes 393224 | tf_op jit(solution)/shard_map/while/body/eval_jaxpr/ppermute | solution.py:12
  389.4 9.9 %collective-permute-start = (f32[128,256]{1,0:T(8,128)S(1)}, f32[128,256]{1,0:T(8,128)S(1)}, u32[]{:S(2)}, u32[]{:S(2)}) collective-permute-start(f32[128,256]{1,0:T(8,128)S(1)} %get-tuple-element.238), channel_id=1, source_target_pairs={{0,16},{16,32},{32,48},{48,64},{64,80},{80,96},{96,112},{112,128},... | collective-permute-start | bytes 393224 | tf_op jit(solution)/shard_map/while/body/eval_jaxpr/ppermute | solution.py:12
  401.1 9.9 %collective-permute-start.1 = (f32[128,256]{1,0:T(8,128)S(1)}, f32[128,256]{1,0:T(8,128)S(1)}, u32[]{:S(2)}, u32[]{:S(2)}) collective-permute-start(f32[128,256]{1,0:T(8,128)S(1)} %get-tuple-element.216), channel_id=1, source_target_pairs={{0,16},{16,32},{32,48},{48,64},{64,80},{80,96},{96,112},{112,128},... | collective-permute-start | bytes 393224 | tf_op jit(solution)/shard_map/while/body/eval_jaxpr/ppermute | solution.py:12
  412.8 9.9 %collective-permute-start = (f32[128,256]{1,0:T(8,128)S(1)}, f32[128,256]{1,0:T(8,128)S(1)}, u32[]{:S(2)}, u32[]{:S(2)}) collective-permute-start(f32[128,256]{1,0:T(8,128)S(1)} %get-tuple-element.238), channel_id=1, source_target_pairs={{0,16},{16,32},{32,48},{48,64},{64,80},{80,96},{96,112},{112,128},... | collective-permute-start | bytes 393224 | tf_op jit(solution)/shard_map/while/body/eval_jaxpr/ppermute | solution.py:12
  424.5 9.9 %collective-permute-start.1 = (f32[128,256]{1,0:T(8,128)S(1)}, f32[128,256]{1,0:T(8,128)S(1)}, u32[]{:S(2)}, u32[]{:S(2)}) collective-permute-start(f32[128,256]{1,0:T(8,128)S(1)} %get-tuple-element.216), channel_id=1, source_target_pairs={{0,16},{16,32},{32,48},{48,64},{64,80},{80,96},{96,112},{112,128},... | collective-permute-start | bytes 393224 | tf_op jit(solution)/shard_map/while/body/eval_jaxpr/ppermute | solution.py:12
  436.2 9.9 %collective-permute-start = (f32[128,256]{1,0:T(8,128)S(1)}, f32[128,256]{1,0:T(8,128)S(1)}, u32[]{:S(2)}, u32[]{:S(2)}) collective-permute-start(f32[128,256]{1,0:T(8,128)S(1)} %get-tuple-element.238), channel_id=1, source_target_pairs={{0,16},{16,32},{32,48},{48,64},{64,80},{80,96},{96,112},{112,128},... | collective-permute-start | bytes 393224 | tf_op jit(solution)/shard_map/while/body/eval_jaxpr/ppermute | solution.py:12
  447.9 9.9 %collective-permute-start.1 = (f32[128,256]{1,0:T(8,128)S(1)}, f32[128,256]{1,0:T(8,128)S(1)}, u32[]{:S(2)}, u32[]{:S(2)}) collective-permute-start(f32[128,256]{1,0:T(8,128)S(1)} %get-tuple-element.216), channel_id=1, source_target_pairs={{0,16},{16,32},{32,48},{48,64},{64,80},{80,96},{96,112},{112,128},... | collective-permute-start | bytes 393224 | tf_op jit(solution)/shard_map/while/body/eval_jaxpr/ppermute | solution.py:12
  459.6 9.9 %collective-permute-start = (f32[128,256]{1,0:T(8,128)S(1)}, f32[128,256]{1,0:T(8,128)S(1)}, u32[]{:S(2)}, u32[]{:S(2)}) collective-permute-start(f32[128,256]{1,0:T(8,128)S(1)} %get-tuple-element.238), channel_id=1, source_target_pairs={{0,16},{16,32},{32,48},{48,64},{64,80},{80,96},{96,112},{112,128},... | collective-permute-start | bytes 393224 | tf_op jit(solution)/shard_map/while/body/eval_jaxpr/ppermute | solution.py:12
  471.3 9.9 %collective-permute-start.1 = (f32[128,256]{1,0:T(8,128)S(1)}, f32[128,256]{1,0:T(8,128)S(1)}, u32[]{:S(2)}, u32[]{:S(2)}) collective-permute-start(f32[128,256]{1,0:T(8,128)S(1)} %get-tuple-element.216), channel_id=1, source_target_pairs={{0,16},{16,32},{32,48},{48,64},{64,80},{80,96},{96,112},{112,128},... | collective-permute-start | bytes 393224 | tf_op jit(solution)/shard_map/while/body/eval_jaxpr/ppermute | solution.py:12
  483.0 9.9 %collective-permute-start = (f32[128,256]{1,0:T(8,128)S(1)}, f32[128,256]{1,0:T(8,128)S(1)}, u32[]{:S(2)}, u32[]{:S(2)}) collective-permute-start(f32[128,256]{1,0:T(8,128)S(1)} %get-tuple-element.238), channel_id=1, source_target_pairs={{0,16},{16,32},{32,48},{48,64},{64,80},{80,96},{96,112},{112,128},... | collective-permute-start | bytes 393224 | tf_op jit(solution)/shard_map/while/body/eval_jaxpr/ppermute | solution.py:12
  494.7 9.9 %collective-permute-start.1 = (f32[128,256]{1,0:T(8,128)S(1)}, f32[128,256]{1,0:T(8,128)S(1)}, u32[]{:S(2)}, u32[]{:S(2)}) collective-permute-start(f32[128,256]{1,0:T(8,128)S(1)} %get-tuple-element.216), channel_id=1, source_target_pairs={{0,16},{16,32},{32,48},{48,64},{64,80},{80,96},{96,112},{112,128},... | collective-permute-start | bytes 393224 | tf_op jit(solution)/shard_map/while/body/eval_jaxpr/ppermute | solution.py:12
  506.4 9.9 %collective-permute-start = (f32[128,256]{1,0:T(8,128)S(1)}, f32[128,256]{1,0:T(8,128)S(1)}, u32[]{:S(2)}, u32[]{:S(2)}) collective-permute-start(f32[128,256]{1,0:T(8,128)S(1)} %get-tuple-element.238), channel_id=1, source_target_pairs={{0,16},{16,32},{32,48},{48,64},{64,80},{80,96},{96,112},{112,128},... | collective-permute-start | bytes 393224 | tf_op jit(solution)/shard_map/while/body/eval_jaxpr/ppermute | solution.py:12
  518.1 9.9 %collective-permute-start.1 = (f32[128,256]{1,0:T(8,128)S(1)}, f32[128,256]{1,0:T(8,128)S(1)}, u32[]{:S(2)}, u32[]{:S(2)}) collective-permute-start(f32[128,256]{1,0:T(8,128)S(1)} %get-tuple-element.216), channel_id=1, source_target_pairs={{0,16},{16,32},{32,48},{48,64},{64,80},{80,96},{96,112},{112,128},... | collective-permute-start | bytes 393224 | tf_op jit(solution)/shard_map/while/body/eval_jaxpr/ppermute | solution.py:12
  529.8 9.9 %collective-permute-start = (f32[128,256]{1,0:T(8,128)S(1)}, f32[128,256]{1,0:T(8,128)S(1)}, u32[]{:S(2)}, u32[]{:S(2)}) collective-permute-start(f32[128,256]{1,0:T(8,128)S(1)} %get-tuple-element.238), channel_id=1, source_target_pairs={{0,16},{16,32},{32,48},{48,64},{64,80},{80,96},{96,112},{112,128},... | collective-permute-start | bytes 393224 | tf_op jit(solution)/shard_map/while/body/eval_jaxpr/ppermute | solution.py:12
  541.5 9.9 %collective-permute-start.1 = (f32[128,256]{1,0:T(8,128)S(1)}, f32[128,256]{1,0:T(8,128)S(1)}, u32[]{:S(2)}, u32[]{:S(2)}) collective-permute-start(f32[128,256]{1,0:T(8,128)S(1)} %get-tuple-element.216), channel_id=1, source_target_pairs={{0,16},{16,32},{32,48},{48,64},{64,80},{80,96},{96,112},{112,128},... | collective-permute-start | bytes 393224 | tf_op jit(solution)/shard_map/while/body/eval_jaxpr/ppermute | solution.py:12
  553.2 9.9 %collective-permute-start = (f32[128,256]{1,0:T(8,128)S(1)}, f32[128,256]{1,0:T(8,128)S(1)}, u32[]{:S(2)}, u32[]{:S(2)}) collective-permute-start(f32[128,256]{1,0:T(8,128)S(1)} %get-tuple-element.238), channel_id=1, source_target_pairs={{0,16},{16,32},{32,48},{48,64},{64,80},{80,96},{96,112},{112,128},... | collective-permute-start | bytes 393224 | tf_op jit(solution)/shard_map/while/body/eval_jaxpr/ppermute | solution.py:12
  564.9 9.9 %collective-permute-start.1 = (f32[128,256]{1,0:T(8,128)S(1)}, f32[128,256]{1,0:T(8,128)S(1)}, u32[]{:S(2)}, u32[]{:S(2)}) collective-permute-start(f32[128,256]{1,0:T(8,128)S(1)} %get-tuple-element.216), channel_id=1, source_target_pairs={{0,16},{16,32},{32,48},{48,64},{64,80},{80,96},{96,112},{112,128},... | collective-permute-start | bytes 393224 | tf_op jit(solution)/shard_map/while/body/eval_jaxpr/ppermute | solution.py:12
  576.6 2.0 copy-start
  578.6 111.9 %copy-start.1 = (f32[32,256]{1,0:T(8,128)S(1)}, f32[32,256]{1,0:T(8,128)}, u32[]{:S(2)}) copy-start(f32[32,256]{1,0:T(8,128)} %param.13) | copy-start | bytes 98308
Sparse Core Ops, SparseCore 0:
  578.7 111.6 reduce-scatter.1
where the time goes:
time: 707 us; the launch traced here: 699 us
  starting transfers between devices  335 us (47%)
  waiting for transfers between devices  188 us (27%)
  blocking collectives  84.8 us (12%)
  matrix products  72.8 us (10%)
  between operations  14.1 us (2%)
    ppermute x40, starting transfers between devices, from_behind(): return lax.ppermute(array, axis, pairs)  335 us
    reduce_scatter x1, waiting for transfers between devices, on_device(): lax.psum_scatter(plain_dot(factor, coupling), 'panel', scatter_dimension=...  112 us
    ppermute x40, waiting for transfers between devices, from_behind(): return lax.ppermute(array, axis, pairs)  76.2 us
    dot_general x80, matrix products, transpose_dot(): lax.dot_general(left, right, (((1,), (1,)), ((), ())), precision=lax.Prec...  70.8 us
    all_gather x1, blocking collectives, on_device(): lax.all_gather(diag_inverse, 'row', axis=0, tiled=True)  34.3 us
    all_gather x1, blocking collectives, on_device(): lax.all_gather(tail_coupling, 'row', axis=0, tiled=True)  26.4 us
    all_gather x1, blocking collectives, on_device(): lax.all_gather(sub_block, 'row', axis=0, tiled=True)  24.1 us
  transfers between devices with their start and end apart: 41, of which 41 were waited for; matrix products, arithmetic and copies ran while one was open for 0% of the time, Pallas kernels for 0%

commit v1 on v0

v1 whole, which is shorter than its diff:
```python
import functools

import jax
import jax.numpy as jnp
from jax import lax
from jax.experimental import pallas as pl
from jax.experimental.pallas import tpu as pltpu
from jax.sharding import PartitionSpec as P

MESH = pl.DeviceIdType.MESH
BATCH = 32
NT = (((1,), (1,)), ((), ()))
NN = (((1,), (0,)), ((), ()))


def split(value):
    high = value.astype(jnp.bfloat16)
    low = (value - high.astype(jnp.float32)).astype(jnp.bfloat16)
    return high, low


def dot3(left, right, dims):
    left_high, left_low = split(left)
    right_high, right_low = split(right)
    dot = functools.partial(lax.dot_general, dimension_numbers=dims, preferred_element_type=jnp.float32)
    return dot(left_high, right_high) + (dot(left_high, right_low) + dot(left_low, right_high))


def kernel(
    panels, rows,
    slab, boundary, inverse_ref, beneath_ref, coupling_ref, cols_ref,
    factor_ref, tail_ref,
    slabs, inverses, beneath, couplings, products, constants, step_high, step_low,
    offset, entering, solved, share, sums_in, sums_out, total,
    z_send, z_recv, x_send, x_recv, pair_send, pair_recv, local_sem,
    y_send, y_recv, s_send, s_recv, t_send, t_recv,
):
    p, r = lax.axis_index("panel"), lax.axis_index("row")
    core = lax.rem(p, 2)
    chip = lax.div(p, 2)
    chips = panels // 2
    z, x = lax.div(r, 2), lax.rem(r, 2)
    depth = rows // 2
    half = slab.shape[0] // 2
    nbatch = half // BATCH
    width = slab.shape[1]
    mine = pl.ds(pl.multiple_of(core * half, half), half)
    other = pl.ds(pl.multiple_of((1 - core) * half, half), half)
    sibling = {"panel": p + 1 - 2 * core, "row": r}
    beside = {"panel": p, "row": r + 1 - 2 * x}
    after = {"panel": p + 2, "row": r}
    ahead = {"panel": p - 2, "row": r}
    collector = {"panel": panels - 2 + lax.div(p, panels // 2), "row": r}
    steps = sorted(range(1, depth), key=lambda d: (min(d, depth - d), d))

    def z_row(shift):
        return lax.rem(z + shift + depth, depth) * 2 + x

    local_slab = pltpu.make_async_copy(slab.at[mine], slabs.at[core], local_sem.at[0])
    local_slab.start()

    barrier = pltpu.get_barrier_semaphore()

    def greet(target):
        pl.semaphore_signal(barrier, inc=1, device_id=target, device_id_type=MESH)

    for shift in steps:
        greet({"panel": p, "row": z_row(shift)})
    greet(beside)
    greet(sibling)
    last = chip == chips - 1

    @pl.when(chip > 0)
    def _():
        greet(ahead)

    @pl.when(p < panels - 1)
    def _():
        greet(collector)

    gathering = jnp.where(last, panels // 2 - core, 1)
    pl.semaphore_wait(barrier, depth + 1 + gathering)

    full = (inverses.at[core], beneath, couplings.at[core])
    shards = (inverse_ref, beneath_ref, coupling_ref)

    def z_copy(k, i, shift):
        return pltpu.make_async_remote_copy(
            src_ref=shards[k], dst_ref=full[k].at[r], send_sem=z_send.at[k, i], recv_sem=z_recv.at[k, i],
            device_id={"panel": p, "row": z_row(shift)}, device_id_type=MESH,
        )

    def z_arrival(k, i, shift):
        return pltpu.make_async_remote_copy(
            src_ref=shards[k], dst_ref=full[k].at[z_row(-shift)], send_sem=z_send.at[k, i], recv_sem=z_recv.at[k, i],
            device_id={"panel": p, "row": z_row(shift)}, device_id_type=MESH,
        )

    def x_own(k):
        return pltpu.make_async_remote_copy(
            src_ref=shards[k], dst_ref=full[k].at[r], send_sem=x_send.at[k, depth - 1], recv_sem=x_recv.at[k, depth - 1],
            device_id=beside, device_id_type=MESH,
        )

    def x_relay(k, i, shift):
        place = full[k].at[z_row(-shift)]
        return pltpu.make_async_remote_copy(
            src_ref=place, dst_ref=place, send_sem=x_send.at[k, i], recv_sem=x_recv.at[k, i],
            device_id=beside, device_id_type=MESH,
        )

    def x_arrivals(k):
        x_own(k).wait_recv()
        for i, shift in enumerate(steps):
            x_relay(k, i, shift).wait_recv()

    def to_sibling(k, src, dst):
        return pltpu.make_async_remote_copy(
            src_ref=src, dst_ref=dst, send_sem=pair_send.at[k], recv_sem=pair_recv.at[k],
            device_id=sibling, device_id_type=MESH,
        )

    pair_slab = to_sibling(0, slab.at[other], slabs.at[core])
    pair_inverse = to_sibling(1, inverses.at[core], inverses.at[core])
    pair_product = to_sibling(2, products.at[core], products.at[core])
    pair_coupling = to_sibling(3, couplings.at[core], couplings.at[core])
    pair_factor = to_sibling(4, solved.at[1 - core], factor_ref.at[mine])

    for k in range(3):
        x_own(k).start()
        for i, shift in enumerate(steps):
            z_copy(k, i, shift).start()
        if k == 0:
            pair_slab.start()
    for k in range(3):
        full[k][r] = shards[k][...]

    def relay(k):
        for i, shift in enumerate(steps):
            z_arrival(k, i, shift).wait_recv()
            x_relay(k, i, shift).start()

    def square(ref):
        return ref[...].reshape(width, width)

    relay(0)
    relay(1)
    x_arrivals(0)
    pair_inverse.start()
    x_arrivals(1)
    products[core] = dot3(square(inverses.at[core]), square(beneath), NN)
    pair_product.start()
    local_slab.wait()
    constants[core] = dot3(slabs[core], square(inverses.at[core]), NT)
    pair_slab.wait_recv()
    pair_inverse.wait_recv()
    constants[1 - core] = dot3(slabs[1 - core], square(inverses.at[1 - core]), NT)
    pair_product.wait_recv()
    step_high[...], step_low[...] = split(dot3(products[1], products[0], NN).T)
    offset[...] = constants[1] - dot3(constants[0], products[1], NT)

    @pl.when(chip == 0)
    def _():
        load = pltpu.make_async_copy(boundary.at[mine], entering, local_sem.at[1])
        load.start()
        load.wait()

    def batch(b):
        return pl.ds(pl.multiple_of(b * BATCH, BATCH), BATCH)

    def y_copy(b):
        return pltpu.make_async_remote_copy(
            src_ref=solved.at[1, batch(b)], dst_ref=entering.at[batch(b)], send_sem=y_send.at[b], recv_sem=y_recv.at[b],
            device_id=after, device_id_type=MESH,
        )

    def advance(b, carry):
        @pl.when(chip > 0)
        def _():
            y_copy(b).wait_recv()

        high, low = split(entering[batch(b)])
        both = jnp.dot(jnp.concatenate([high, low], axis=0), step_high[...], preferred_element_type=jnp.float32)
        rest = jnp.dot(high, step_low[...], preferred_element_type=jnp.float32)
        solved[1, batch(b)] = offset[batch(b)] + (both[:BATCH] + (both[BATCH:] + rest))

        @pl.when(chip < chips - 1)
        def _():
            y_copy(b).start()

        return carry

    lax.fori_loop(0, nbatch // 2, advance, 0)
    relay(2)
    lax.fori_loop(nbatch // 2, nbatch, advance, 0)
    x_arrivals(2)
    pair_coupling.start()
    solved[0] = constants[0] - dot3(entering[...], products[0], NT)
    pair_factor.start()
    share[...] = dot3(solved[core], square(couplings.at[core]), NN)
    factor_ref[mine] = solved[core]
    pair_coupling.wait_recv()
    share[...] += dot3(solved[1 - core], square(couplings.at[1 - core]), NN)

    def s_copy(b):
        return pltpu.make_async_remote_copy(
            src_ref=sums_out.at[batch(b)], dst_ref=sums_in.at[batch(b)], send_sem=s_send.at[b], recv_sem=s_recv.at[b],
            device_id=after, device_id_type=MESH,
        )

    def t_copy(b):
        return pltpu.make_async_remote_copy(
            src_ref=sums_out.at[batch(b)], dst_ref=total, send_sem=t_send.at[b], recv_sem=t_recv.at[0],
            device_id={"panel": core * nbatch + b, "row": r}, device_id_type=MESH,
        )

    def add_up(b, carry):
        @pl.when(chip == 0)
        def _():
            sums_out[batch(b)] = share[batch(b)]

        @pl.when(chip > 0)
        def _():
            s_copy(b).wait_recv()
            sums_out[batch(b)] = sums_in[batch(b)] + share[batch(b)]

        @pl.when(chip < chips - 1)
        def _():
            s_copy(b).start()

        owner = core * nbatch + b

        @pl.when(last & (owner != p))
        def _():
            t_copy(b).start()

        @pl.when(last & (owner == p))
        def _():
            total[...] = sums_out[batch(b)]

        return carry

    lax.fori_loop(0, nbatch, add_up, 0)

    @pl.when(p < panels - 1)
    def _():
        t_copy(0).wait_recv()

    tail_ref[...] = cols_ref[...] - total[...]

    def drain(b, carry):
        @pl.when(chip < chips - 1)
        def _():
            y_copy(b).wait_send()
            s_copy(b).wait_send()

        @pl.when(last & (core * nbatch + b != p))
        def _():
            t_copy(b).wait_send()

        return carry

    lax.fori_loop(0, nbatch, drain, 0)
    for k in range(3):
        x_own(k).wait_send()
        for i, shift in enumerate(steps):
            z_copy(k, i, shift).wait_send()
            x_relay(k, i, shift).wait_send()
    pair_slab.wait_send()
    pair_inverse.wait_send()
    pair_product.wait_send()
    pair_coupling.wait_send()
    pair_factor.wait()


def solution(mesh):
    panels, rows = mesh.shape["panel"], mesh.shape["row"]

    def on_device(slab, boundary, diag_inverse, sub_block, tail_coupling, tail_cols):
        height, width = slab.shape
        half = height // 2
        depth = rows // 2
        nbatch = half // BATCH
        f32 = jnp.float32
        shard = diag_inverse.shape[0]
        whole = pl.BlockSpec(memory_space=pltpu.VMEM)
        apart = pl.BlockSpec(memory_space=pl.ANY)
        dma = pltpu.SemaphoreType.DMA
        return pl.pallas_call(
            functools.partial(kernel, panels, rows),
            out_shape=(
                jax.ShapeDtypeStruct((height, width), f32),
                jax.ShapeDtypeStruct(tail_cols.shape, f32),
            ),
            in_specs=[apart, apart, whole, whole, whole, whole],
            out_specs=(whole, whole),
            scratch_shapes=[
                pltpu.VMEM((2, half, width), f32),
                pltpu.VMEM((2, rows, shard, width), f32),
                pltpu.VMEM((rows, shard, width), f32),
                pltpu.VMEM((2, rows, shard, width), f32),
                pltpu.VMEM((2, width, width), f32),
                pltpu.VMEM((2, half, width), f32),
                pltpu.VMEM((width, width), jnp.bfloat16),
                pltpu.VMEM((width, width), jnp.bfloat16),
                pltpu.VMEM((half, width), f32),
                pltpu.VMEM((half, width), f32),
                pltpu.VMEM((2, half, width), f32),
                pltpu.VMEM((half, width), f32),
                pltpu.VMEM((half, width), f32),
                pltpu.VMEM((half, width), f32),
                pltpu.VMEM((BATCH, width), f32),
                dma((3, depth - 1)),
                dma((3, depth - 1)),
                dma((3, depth)),
                dma((3, depth)),
                dma((5,)),
                dma((5,)),
                dma((2,)),
                dma((nbatch,)),
                dma((nbatch,)),
                dma((nbatch,)),
                dma((nbatch,)),
                dma((nbatch,)),
                dma((1,)),
            ],
            compiler_params=pltpu.CompilerParams(
                collective_id=0, has_side_effects=True, vmem_limit_bytes=48 << 20
            ),
        )(slab, boundary, diag_inverse, sub_block, tail_coupling, tail_cols)

    placed = (
        P("row", "panel"),
        P("row", None),
        P(("panel", "row"), None),
        P(("panel", "row"), None),
        P(("panel", "row"), None),
        P(("row", "panel"), None),
    )
    return jax.shard_map(
        on_device,
        mesh=mesh,
        in_specs=placed,
        out_specs=(P("row", "panel"), P(("row", "panel"), None)),
        check_vma=False,
    )
```

time: 707 us -> 109 us (0.15); the launches traced: 699 us -> 109 us
  starting transfers between devices: 335 us -> 0 us
  waiting for transfers between devices: 188 us -> 0 us
  Pallas kernels: 0 us -> 101 us
  blocking collectives: 84.8 us -> 0 us
  matrix products: 72.8 us -> 0 us
  between operations: 14.1 us -> 0.65 us
    ppermute x40 -> x0, starting transfers between devices: 335 us -> none  [from_behind(): return lax.ppermute(array, axis, pairs)]
    reduce_scatter x1 -> x0, waiting for transfers between devices: 112 us -> none  [on_device(): lax.psum_scatter(plain_dot(factor, coupling), 'panel', scatter_dimension=...]
    pallas_call x0 -> x1, Pallas kernels: none -> 101 us  [on_device(): pl.pallas_call(functools.partial(kernel, panels, rows), out_shape=(jax.Sh...]
    all_gather x3 -> x0, blocking collectives: 84.8 us -> none  [the longest x1 34.3 us: on_device(): lax.all_gather(diag_inverse, 'row', axis=0, tiled=True)]
    ppermute x40 -> x0, waiting for transfers between devices: 76.2 us -> none  [from_behind(): return lax.ppermute(array, axis, pairs)]
    dot_general x81 -> x0, matrix products: 72.8 us -> none  [the longest x80 70.8 us: transpose_dot(): lax.dot_general(left, right, (((1,), (1,)), ((), ())), precision=lax.Prec...]
  transfers between devices with their start and end apart: 41 -> 0, of which waited for: 41 -> 0; matrix products, arithmetic and copies ran while one was open for 0% -> 0% of each run, Pallas kernels for 0% -> 0%
where the time goes in v1:
time: 109 us
  Pallas kernels  101 us (93%)
  local copies, waits for them, and re-layouts  6.94 us (6%)
    pallas_call x1, Pallas kernels, on_device(): pl.pallas_call(functools.partial(kernel, panels, rows), out_shape=(jax.Sh...  101 us
    unnamed x14, local copies, waits for them, and re-layouts  6.94 us

profile of v1, /device:TPU:57, one launch (start us, length us, event | category | flops | bytes accessed | tf_op | source)
XLA Modules:
  0.0 108.6 jit_solution(17688259544056624082)
XLA Ops:
  0.6 0.0 copy-start
  0.6 1.2 %copy-done = f32[1024,256]{1,0:T(8,128)S(1)} copy-done((f32[1024,256]{1,0:T(8,128)S(1)}, f32[1024,256]{1,0:T(8,128)}, u32[]{:S(2)}) %copy-start) | copy-done | bytes 1048600
  1.9 0.0 copy-start.1
  1.9 1.2 %copy-done.1 = f32[1024,256]{1,0:T(8,128)S(1)} copy-done((f32[1024,256]{1,0:T(8,128)S(1)}, f32[1024,256]{1,0:T(8,128)}, u32[]{:S(2)}) %copy-start.1) | copy-done | bytes 1048600
  3.1 0.0 copy-start.2
  3.1 0.8 copy-done.2
  3.8 0.0 copy-start.3
  3.8 0.7 copy-done.3
  4.6 0.0 copy-start.4
  4.6 0.7 copy-done.4
  5.3 0.0 copy-start.5
  5.3 0.7 copy-done.5
  6.0 101.0 %shard_map.77 = (f32[1024,256]{1,0:T(8,128)S(1)}, f32[32,256]{1,0:T(8,128)S(1)}) custom-call(f32[1024,256]{1,0:T(8,128)S(1)} %copy-done, f32[1024,256]{1,0:T(8,128)S(1)} %copy-done.1, f32[16,256]{1,0:T(8,128)S(1)} %copy-done.3, f32[16,256]{1,0:T(8,128)S(1)} %copy-done.4, f32[16,256]{1,0:T(8,128)S(1)} %copy-done.5, f32[32,256]{1,0:T(8,128)S(1)} %copy-done.2), custom_call_target="tpu_custom_call" | custom-call | tf_op jit(solution)/shard_map/pallas_call | solution.py:289
  107.0 1.0 copy.10
  108.0 0.6 copy.11
Async XLA Ops:
  0.6 1.2 %copy-start = (f32[1024,256]{1,0:T(8,128)S(1)}, f32[1024,256]{1,0:T(8,128)}, u32[]{:S(2)}) copy-start(f32[1024,256]{1,0:T(8,128)} %slab.1) | copy-start | bytes 3145732
  1.9 1.2 %copy-start.1 = (f32[1024,256]{1,0:T(8,128)S(1)}, f32[1024,256]{1,0:T(8,128)}, u32[]{:S(2)}) copy-start(f32[1024,256]{1,0:T(8,128)} %boundary.1) | copy-start | bytes 3145732
  3.1 0.8 copy-start.2
  3.8 0.7 copy-start.3
  4.6 0.7 copy-start.4
  5.3 0.7 copy-start.5

commit v2 on v1

--- a/solution.py
+++ b/solution.py
@@ -9,6 +9,7 @@
 
 MESH = pl.DeviceIdType.MESH
 BATCH = 32
+PIECE = 16
 NT = (((1,), (1,)), ((), ()))
 NN = (((1,), (0,)), ((), ()))
 
@@ -31,7 +32,7 @@
     slab, boundary, inverse_ref, beneath_ref, coupling_ref, cols_ref,
     factor_ref, tail_ref,
     slabs, inverses, beneath, couplings, products, constants, step_high, step_low,
-    offset, entering, solved, share, sums_in, sums_out, total,
+    offset, entering, solved, share, sums_in, sums_out, total, cols,
     z_send, z_recv, x_send, x_recv, pair_send, pair_recv, local_sem,
     y_send, y_recv, s_send, s_recv, t_send, t_recv,
 ):
@@ -58,6 +59,13 @@
 
     local_slab = pltpu.make_async_copy(slab.at[mine], slabs.at[core], local_sem.at[0])
     local_slab.start()
+    local_cols = pltpu.make_async_copy(cols_ref, cols, local_sem.at[2])
+    local_cols.start()
+    full = (inverses.at[core], beneath, couplings.at[core])
+    shards = (inverse_ref, beneath_ref, coupling_ref)
+    local_shards = [pltpu.make_async_copy(shards[k], full[k].at[r], local_sem.at[3 + k]) for k in range(3)]
+    for copy in local_shards:
+        copy.start()
 
     barrier = pltpu.get_barrier_semaphore()
 
@@ -80,9 +88,6 @@
 
     gathering = jnp.where(last, panels // 2 - core, 1)
     pl.semaphore_wait(barrier, depth + 1 + gathering)
-
-    full = (inverses.at[core], beneath, couplings.at[core])
-    shards = (inverse_ref, beneath_ref, coupling_ref)
 
     def z_copy(k, i, shift):
         return pltpu.make_async_remote_copy(
@@ -132,8 +137,8 @@
             z_copy(k, i, shift).start()
         if k == 0:
             pair_slab.start()
-    for k in range(3):
-        full[k][r] = shards[k][...]
+    for copy in local_shards:
+        copy.wait()
 
     def relay(k):
         for i, shift in enumerate(steps):
@@ -168,9 +173,12 @@
     def batch(b):
         return pl.ds(pl.multiple_of(b * BATCH, BATCH), BATCH)
 
+    def piece(b):
+        return pl.ds(pl.multiple_of(b * PIECE, PIECE), PIECE)
+
     def y_copy(b):
         return pltpu.make_async_remote_copy(
-            src_ref=solved.at[1, batch(b)], dst_ref=entering.at[batch(b)], send_sem=y_send.at[b], recv_sem=y_recv.at[b],
+            src_ref=solved.at[1, piece(b)], dst_ref=entering.at[piece(b)], send_sem=y_send.at[b], recv_sem=y_recv.at[b],
             device_id=after, device_id_type=MESH,
         )
 
@@ -179,10 +187,10 @@
         def _():
             y_copy(b).wait_recv()
 
-        high, low = split(entering[batch(b)])
+        high, low = split(entering[piece(b)])
         both = jnp.dot(jnp.concatenate([high, low], axis=0), step_high[...], preferred_element_type=jnp.float32)
         rest = jnp.dot(high, step_low[...], preferred_element_type=jnp.float32)
-        solved[1, batch(b)] = offset[batch(b)] + (both[:BATCH] + (both[BATCH:] + rest))
+        solved[1, piece(b)] = offset[piece(b)] + (both[:PIECE] + (both[PIECE:] + rest))
 
         @pl.when(chip < chips - 1)
         def _():
@@ -190,9 +198,10 @@
 
         return carry
 
-    lax.fori_loop(0, nbatch // 2, advance, 0)
+    npiece = half // PIECE
+    lax.fori_loop(0, npiece // 2, advance, 0)
     relay(2)
-    lax.fori_loop(nbatch // 2, nbatch, advance, 0)
+    lax.fori_loop(npiece // 2, npiece, advance, 0)
     x_arrivals(2)
     pair_coupling.start()
     solved[0] = constants[0] - dot3(entering[...], products[0], NT)
@@ -246,21 +255,30 @@
     def _():
         t_copy(0).wait_recv()
 
-    tail_ref[...] = cols_ref[...] - total[...]
+    local_cols.wait()
+    tail_ref[...] = cols[...] - total[...]
 
     def drain(b, carry):
         @pl.when(chip < chips - 1)
         def _():
+            s_copy(b).wait_send()
+
+        @pl.when(last & (core * nbatch + b != p))
+        def _():
+            t_copy(b).wait_send()
+
+        return carry
+
+    lax.fori_loop(0, nbatch, drain, 0)
+
+    def drain_steps(b, carry):
+        @pl.when(chip < chips - 1)
+        def _():
             y_copy(b).wait_send()
-            s_copy(b).wait_send()
-
-        @pl.when(last & (core * nbatch + b != p))
-        def _():
-            t_copy(b).wait_send()
 
         return carry
 
-    lax.fori_loop(0, nbatch, drain, 0)
+    lax.fori_loop(0, npiece, drain_steps, 0)
     for k in range(3):
         x_own(k).wait_send()
         for i, shift in enumerate(steps):
@@ -284,15 +302,19 @@
         f32 = jnp.float32
         shard = diag_inverse.shape[0]
         whole = pl.BlockSpec(memory_space=pltpu.VMEM)
-        apart = pl.BlockSpec(memory_space=pl.ANY)
+        apart = pl.BlockSpec(memory_space=pltpu.HBM)
         dma = pltpu.SemaphoreType.DMA
+        operands = [
+            pltpu.with_memory_space_constraint(value, pltpu.HBM)
+            for value in (slab, boundary, diag_inverse, sub_block, tail_coupling, tail_cols)
+        ]
         return pl.pallas_call(
             functools.partial(kernel, panels, rows),
             out_shape=(
                 jax.ShapeDtypeStruct((height, width), f32),
                 jax.ShapeDtypeStruct(tail_cols.shape, f32),
             ),
-            in_specs=[apart, apart, whole, whole, whole, whole],
+            in_specs=[apart, apart, apart, apart, apart, apart],
             out_specs=(whole, whole),
             scratch_shapes=[
                 pltpu.VMEM((2, half, width), f32),
@@ -310,15 +332,16 @@
                 pltpu.VMEM((half, width), f32),
                 pltpu.VMEM((half, width), f32),
                 pltpu.VMEM((BATCH, width), f32),
+                pltpu.VMEM(tail_cols.shape, f32),
                 dma((3, depth - 1)),
                 dma((3, depth - 1)),
                 dma((3, depth)),
                 dma((3, depth)),
                 dma((5,)),
                 dma((5,)),
-                dma((2,)),
-                dma((nbatch,)),
-                dma((nbatch,)),
+                dma((6,)),
+                dma((half // PIECE,)),
+                dma((half // PIECE,)),
                 dma((nbatch,)),
                 dma((nbatch,)),
                 dma((nbatch,)),
@@ -327,7 +350,7 @@
             compiler_params=pltpu.CompilerParams(
                 collective_id=0, has_side_effects=True, vmem_limit_bytes=48 << 20
             ),
-        )(slab, boundary, diag_inverse, sub_block, tail_coupling, tail_cols)
+        )(*operands)
 
     placed = (
         P("row", "panel"),

time: 109 us -> 102 us (0.936)
  local copies, waits for them, and re-layouts: 6.94 us -> 1.59 us
  Pallas kernels: 101 us -> 99.6 us
    unnamed x14 -> x2, local copies, waits for them, and re-layouts: 6.94 us -> 1.59 us
    pallas_call x1, Pallas kernels: 101 us -> 99.6 us  [on_device(): pl.pallas_call(functools.partial(kernel, panels, rows), out_shape=(jax.Sh...]
where the time goes in v2:
time: 102 us
  Pallas kernels  99.6 us (98%)
  local copies, waits for them, and re-layouts  1.59 us (2%)
    pallas_call x1, Pallas kernels, on_device(): pl.pallas_call(functools.partial(kernel, panels, rows), out_shape=(jax.Sh...  99.6 us

profile of v2, /device:TPU:57, one launch (start us, length us, event | category | flops | bytes accessed | tf_op | source)
XLA Modules:
  0.0 101.9 jit_solution(8555220836206823651)
XLA Ops:
  0.6 99.6 %shard_map.77 = (f32[1024,256]{1,0:T(8,128)S(1)}, f32[32,256]{1,0:T(8,128)S(1)}) custom-call(f32[1024,256]{1,0:T(8,128)} %slab.1, f32[1024,256]{1,0:T(8,128)} %boundary.1, f32[16,256]{1,0:T(8,128)} %inverse_ref.1, f32[16,256]{1,0:T(8,128)} %beneath_ref.1, f32[16,256]{1,0:T(8,128)} %coupling_ref.1, f32[32,256]{1,0:T(8,128)} %cols_ref.1), custom_call_target="tpu_custom_call" | custom-call | tf_op jit(solution)/shard_map/pallas_call | solution.py:311
  100.3 1.0 copy.10
  101.3 0.6 copy.11

commit v3 on v2

v3 whole, which is shorter than its diff:
```python
import functools

import jax
import jax.numpy as jnp
from jax import lax
from jax.experimental import pallas as pl
from jax.experimental.pallas import tpu as pltpu
from jax.sharding import PartitionSpec as P

MESH = pl.DeviceIdType.MESH
STEP = 32
GROUP = 4
NT = (((1,), (1,)), ((), ()))
NN = (((1,), (0,)), ((), ()))


def split(value):
    high = value.astype(jnp.bfloat16)
    low = (value - high.astype(jnp.float32)).astype(jnp.bfloat16)
    return high, low


def dot3(left, right, dims):
    left_high, left_low = split(left)
    right_high, right_low = split(right)
    dot = functools.partial(lax.dot_general, dimension_numbers=dims, preferred_element_type=jnp.float32)
    return dot(left_high, right_high) + (dot(left_high, right_low) + dot(left_low, right_high))


def kernel(
    panels, rows,
    slab, boundary, inverse_ref, beneath_ref, coupling_ref, cols_ref,
    factor_ref, tail_ref,
    slabs, inverses, beneath, couplings, products, constants, offset, entering, solved,
    sums_in, sums_out, inflow, passed, carry, carry_even, carry_sum, weight_high, weight_low, share, total, cols,
    z_send, z_recv, x_send, x_recv, g_send, g_recv, pair_send, pair_recv, local_sem,
    y_send, y_recv, t_send, t_recv, in_send, in_recv, lead_send, relay_send, u_send, u_recv,
):
    p, r = lax.axis_index("panel"), lax.axis_index("row")
    core = lax.rem(p, 2)
    chip = lax.div(p, 2)
    chips = panels // 2
    groups = chips // GROUP
    group, spot = lax.div(chip, GROUP), lax.rem(chip, GROUP)
    side = lax.div(p, panels // 2)
    z, x = lax.div(r, 2), lax.rem(r, 2)
    depth = rows // 2
    half = slab.shape[0] // 2
    width = slab.shape[1]
    head = width // 2
    n_head, n_data = head // STEP, half // STEP
    n_all = n_head + n_data
    body = pl.ds(head, half)
    mine = pl.ds(pl.multiple_of(core * half, half), half)
    other = pl.ds(pl.multiple_of((1 - core) * half, half), half)
    steps = sorted(range(1, depth), key=lambda d: (min(d, depth - d), d))

    first, final = spot == 0, spot == GROUP - 1
    carried = group > 0
    feeds = final & (group < groups - 1)

    def at(panel):
        return {"panel": panel, "row": r}

    sibling = at(p + 1 - 2 * core)
    beside = {"panel": p, "row": r + 1 - 2 * x}
    after, ahead = at(p + 2), at(p - 2)
    skip_after, skip_ahead = at(p + 2 * GROUP), at(p - 2 * GROUP)
    source_panels = [2 * (GROUP * k + GROUP - 1) for k in range(groups)]

    def z_row(shift):
        return lax.rem(z + shift + depth, depth) * 2 + x

    def any_row(shift):
        return lax.rem(r + shift + rows, rows)

    local_slab = pltpu.make_async_copy(slab.at[mine], slabs.at[core], local_sem.at[0])
    local_slab.start()
    local_cols = pltpu.make_async_copy(cols_ref, cols, local_sem.at[1])
    local_cols.start()
    local_boundary = pltpu.make_async_copy(boundary.at[mine], entering.at[body], local_sem.at[2])

    @pl.when(chip == 0)
    def _():
        local_boundary.start()

    full = (inverses.at[core], beneath, couplings.at[core])
    shards = (inverse_ref, beneath_ref, coupling_ref)
    local_shards = [pltpu.make_async_copy(shards[k], full[k].at[r], local_sem.at[3 + k]) for k in range(3)]
    for copy in local_shards:
        copy.start()

    barrier = pltpu.get_barrier_semaphore()

    def greet(target):
        pl.semaphore_signal(barrier, inc=1, device_id=target, device_id_type=MESH)

    for shift in range(1, rows):
        greet({"panel": p, "row": any_row(shift)})
    greet(sibling)

    @pl.when(chip > 0)
    def _():
        greet(ahead)

    @pl.when(carried & (spot == GROUP - 2))
    def _():
        greet(after)

    @pl.when(final & carried)
    def _():
        greet(skip_ahead)

    for start in source_panels:
        @pl.when(start + side != p)
        def _():
            greet(at(start + side))

    expected = (
        rows + jnp.where(chip < chips - 1, 1, 0) + jnp.where(carried & final, 1, 0) + jnp.where(feeds, 1, 0)
        + jnp.where(final, jnp.where(side == core, n_data - 1, n_data), 0)
    )
    pl.semaphore_wait(barrier, expected)

    def remote(src, dst, send, recv, target):
        return pltpu.make_async_remote_copy(
            src_ref=src, dst_ref=dst, send_sem=send, recv_sem=recv, device_id=target, device_id_type=MESH
        )

    def z_copy(k, i, shift, place):
        return remote(
            shards[k], full[k].at[place], z_send.at[k, i], z_recv.at[k, i], {"panel": p, "row": z_row(shift)}
        )

    def x_own(k):
        return remote(shards[k], full[k].at[r], x_send.at[k, depth - 1], x_recv.at[k, depth - 1], beside)

    def x_relay(k, i, shift):
        place = full[k].at[z_row(-shift)]
        return remote(place, place, x_send.at[k, i], x_recv.at[k, i], beside)

    def g_copy(shift, place):
        return remote(
            shards[2], full[2].at[place], g_send.at[shift - 1], g_recv.at[shift - 1],
            {"panel": p, "row": any_row(shift)},
        )

    def to_sibling(k, src, dst):
        return remote(src, dst, pair_send.at[k], pair_recv.at[k], sibling)

    pair_slab = to_sibling(0, slab.at[other], slabs.at[core])
    pair_inverse = to_sibling(1, inverses.at[core], inverses.at[core])
    pair_product = to_sibling(2, products.at[core], products.at[core])
    pair_coupling = to_sibling(3, couplings.at[core], couplings.at[core])
    pair_carry = to_sibling(4, solved.at[1, pl.ds(0, head)], carry.at[core])
    pair_even = to_sibling(5, solved.at[0, pl.ds(0, head)], carry_even.at[core])
    pair_sum = to_sibling(6, sums_out.at[pl.ds(0, head)], carry_sum.at[core])
    pair_factor = to_sibling(7, solved.at[1 - core, body], factor_ref.at[mine])

    for k in range(2):
        x_own(k).start()
        for i, shift in enumerate(steps):
            z_copy(k, i, shift, r).start()
        if k == 0:
            pair_slab.start()
    for shift in range(1, rows):
        g_copy(shift, r).start()
    for copy in local_shards:
        copy.wait()

    def relay(k):
        for i, shift in enumerate(steps):
            z_copy(k, i, shift, z_row(-shift)).wait_recv()
            x_relay(k, i, shift).start()

    def x_arrivals(k):
        x_own(k).wait_recv()
        for i, shift in enumerate(steps):
            x_relay(k, i, shift).wait_recv()

    def square(ref):
        return ref[...].reshape(width, width)

    def keep(k, value):
        weight_high[k], weight_low[k] = split(value)

    def times(value, k):
        high, low = split(value)
        count = value.shape[0]
        both = jnp.dot(jnp.concatenate([high, low], axis=0), weight_high[k], preferred_element_type=jnp.float32)
        rest = jnp.dot(high, weight_low[k], preferred_element_type=jnp.float32)
        return both[:count] + (both[count:] + rest)

    zeros = jnp.zeros((head, width), jnp.float32)
    offset[:head] = zeros
    constants[0, :head] = zeros

    @pl.when(first)
    def _():
        row = lax.broadcasted_iota(jnp.int32, (head, width), 0) + core * head
        column = lax.broadcasted_iota(jnp.int32, (head, width), 1)
        entering[:head] = jnp.where(row == column, 1.0, 0.0)

    @pl.when(first & carried)
    def _():
        entering[body] = jnp.zeros((half, width), jnp.float32)

    relay(0)
    relay(1)
    x_arrivals(0)
    pair_inverse.start()
    x_arrivals(1)
    products[core] = dot3(square(inverses.at[core]), square(beneath), NN)
    pair_product.start()
    local_slab.wait()
    constants[core, body] = dot3(slabs[core], square(inverses.at[core]), NT)
    pair_slab.wait_recv()
    pair_inverse.wait_recv()
    constants[1 - core, body] = dot3(slabs[1 - core], square(inverses.at[1 - core]), NT)
    pair_product.wait_recv()
    keep(0, dot3(products[1], products[0], NN).T)
    offset[body] = constants[1, body] - dot3(constants[0, body], products[1], NT)
    keep(1, products[0].T)

    @pl.when(chip == 0)
    def _():
        local_boundary.wait()

    def batch(b):
        return pl.ds(pl.multiple_of(b * STEP, STEP), STEP)

    def data(b):
        return pl.ds(pl.multiple_of(b * STEP + head, STEP), STEP)

    def y_copy(b):
        return remote(solved.at[1, batch(b)], entering.at[batch(b)], y_send.at[b], y_recv.at[b], after)

    def t_copy(b):
        return remote(sums_out.at[batch(b)], sums_in.at[batch(b)], t_send.at[b], t_recv.at[b], after)

    def in_copy(b):
        return remote(passed.at[batch(b)], inflow.at[batch(b)], in_send.at[b], in_recv.at[b], skip_after)

    def lead_copy(b):
        return remote(passed.at[batch(b)], inflow.at[batch(b)], lead_send.at[b], in_recv.at[b], after)

    def back_copy(b):
        return remote(inflow.at[batch(b)], inflow.at[batch(b)], relay_send.at[b], in_recv.at[b], ahead)

    def forth_copy(b):
        return remote(inflow.at[batch(b)], inflow.at[batch(b)], relay_send.at[b], in_recv.at[b], after)

    def u_copy(b):
        return remote(
            share.at[batch(b)], total.at[group], u_send.at[b], u_recv.at[group], at(core * n_data + b)
        )

    begin = jnp.where(carried, 0, n_head)
    couple_turn = n_all - 4
    inflow_lag = jnp.where(final, 7 * group, 2 * n_all)
    sum_lag = jnp.where(feeds & carried, inflow_lag + n_data, n_all)
    share_lag = sum_lag + n_head + 4
    turns = 2 * n_all + n_data

    def turn(i, unused):
        @pl.when((i >= begin) & (i < n_all))
        def _():
            @pl.when(spot > 0)
            def _():
                y_copy(i).wait_recv()

            row = offset[batch(i)] + times(entering[batch(i)], 0)
            solved[1, batch(i)] = row

            @pl.when(spot < GROUP - 1)
            def _():
                y_copy(i).start()

            @pl.when(final & (group == 0))
            def _():
                passed[batch(i - n_head)] = row
                in_copy(i - n_head).start()
                lead_copy(i - n_head).start()

        @pl.when(carried & (i == n_head))
        def _():
            pair_carry.start()
            carry[core] = solved[1, :head]

        @pl.when(i == couple_turn)
        def _():
            for shift in range(1, rows):
                g_copy(shift, any_row(-shift)).wait_recv()
            pair_coupling.start()

        @pl.when(i == sum_lag)
        def _():
            pair_coupling.wait_recv()
            keep(2, square(couplings.at[0]))
            keep(3, square(couplings.at[1]))

        b = i - sum_lag

        @pl.when((b >= begin) & (b < n_all))
        def _():
            even = constants[0, batch(b)] - times(entering[batch(b)], 1)
            solved[0, batch(b)] = even
            part = times(even, 2) + times(solved[1, batch(b)], 3)

            @pl.when(first)
            def _():
                sums_out[batch(b)] = part

            @pl.when(spot > 0)
            def _():
                t_copy(b).wait_recv()
                sums_out[batch(b)] = sums_in[batch(b)] + part

            @pl.when(spot < GROUP - 1)
            def _():
                t_copy(b).start()

        @pl.when(carried & (b == n_head))
        def _():
            pair_even.start()
            carry_even[core] = solved[0, :head]

        @pl.when(carried & final & (b == n_head))
        def _():
            pair_sum.start()
            carry_sum[core] = sums_out[:head]

        @pl.when(carried & final & (i == inflow_lag))
        def _():
            pair_carry.wait_recv()
            keep(4, carry[...].reshape(width, width))

        m = i - inflow_lag

        @pl.when(carried & (first | final) & (m >= 0) & (m < n_data))
        def _():
            in_copy(m).wait_recv()

            @pl.when(first)
            def _():
                forth_copy(m).start()

            @pl.when(final & jnp.logical_not(feeds))
            def _():
                back_copy(m).start()

            @pl.when(final)
            def _():
                passed[batch(m)] = solved[1, data(m)] + times(inflow[batch(m)], 4)

            @pl.when(feeds)
            def _():
                in_copy(m).start()
                lead_copy(m).start()

        @pl.when(carried & feeds & (m == n_data))
        def _():
            def hand_back(k, unused):
                back_copy(k).start()
                return unused

            lax.fori_loop(0, n_data, hand_back, 0)

        @pl.when(carried & final & (i == share_lag))
        def _():
            pair_sum.wait_recv()
            keep(6, carry_sum[...].reshape(width, width))

        t = i - share_lag

        @pl.when(final & (t >= 0) & (t < n_data))
        def _():
            @pl.when(carried)
            def _():
                share[batch(t)] = sums_out[data(t)] + times(inflow[batch(t)], 6)

            @pl.when(group == 0)
            def _():
                share[batch(t)] = sums_out[data(t)]

            @pl.when(core * n_data + t != p)
            def _():
                u_copy(t).start()

            @pl.when(core * n_data + t == p)
            def _():
                total[group] = share[batch(t)]

        return unused

    lax.fori_loop(0, turns, turn, 0)

    @pl.when(final & carried)
    def _():
        solved[1, body] = passed[...]

    @pl.when(spot < GROUP - 1)
    def _():
        def sent(b, unused):
            y_copy(b).wait_send()
            t_copy(b).wait_send()
            return unused

        lax.fori_loop(begin, n_all, sent, 0)

    @pl.when(carried & (spot > 0) & (spot < GROUP - 1))
    def _():
        def reached(b, unused):
            in_copy(b).wait_recv()
            return unused

        lax.fori_loop(0, n_data, reached, 0)

    @pl.when(carried & (spot < GROUP - 1))
    def _():
        pair_carry.wait_recv()
        keep(4, carry[...].reshape(width, width))
        solved[1, body] += times(inflow[...], 4)

    @pl.when(carried)
    def _():
        pair_even.wait_recv()
        keep(5, carry_even[...].reshape(width, width))
        solved[0, body] += times(inflow[...], 5)

    pair_factor.start()
    factor_ref[mine] = solved[core, body]

    for k, start in enumerate(source_panels):
        @pl.when(start + side != p)
        def _():
            remote(share.at[batch(0)], total.at[k], u_send.at[0], u_recv.at[k], at(start + side)).wait_recv()

    local_cols.wait()
    summed = total[0]
    for k in range(1, groups):
        summed = summed + total[k]
    tail_ref[...] = cols[...] - summed

    def drain(b, unused):
        @pl.when(feeds)
        def _():
            in_copy(b).wait_send()
            lead_copy(b).wait_send()

        @pl.when(carried & (first | final))
        def _():
            back_copy(b).wait_send()

        @pl.when(final & (core * n_data + b != p))
        def _():
            u_copy(b).wait_send()

        return unused

    lax.fori_loop(0, n_data, drain, 0)

    for k in range(2):
        x_own(k).wait_send()
        for i, shift in enumerate(steps):
            z_copy(k, i, shift, r).wait_send()
            x_relay(k, i, shift).wait_send()
    for shift in range(1, rows):
        g_copy(shift, r).wait_send()
    pair_slab.wait_send()
    pair_inverse.wait_send()
    pair_product.wait_send()
    pair_coupling.wait_send()

    @pl.when(carried)
    def _():
        pair_carry.wait_send()
        pair_even.wait_send()

    @pl.when(carried & final)
    def _():
        pair_sum.wait_send()

    pair_factor.wait()


def solution(mesh):
    panels, rows = mesh.shape["panel"], mesh.shape["row"]

    def on_device(slab, boundary, diag_inverse, sub_block, tail_coupling, tail_cols):
        height, width = slab.shape
        half, head = height // 2, width // 2
        extended = head + half
        depth = rows // 2
        n_data, n_all = half // STEP, extended // STEP
        groups = panels // 2 // GROUP
        f32, bf16 = jnp.float32, jnp.bfloat16
        shard = diag_inverse.shape[0]
        whole = pl.BlockSpec(memory_space=pltpu.VMEM)
        apart = pl.BlockSpec(memory_space=pltpu.HBM)
        dma = pltpu.SemaphoreType.DMA
        operands = [
            pltpu.with_memory_space_constraint(value, pltpu.HBM)
            for value in (slab, boundary, diag_inverse, sub_block, tail_coupling, tail_cols)
        ]
        return pl.pallas_call(
            functools.partial(kernel, panels, rows),
            out_shape=(
                jax.ShapeDtypeStruct((height, width), f32),
                jax.ShapeDtypeStruct(tail_cols.shape, f32),
            ),
            in_specs=[apart] * 6,
            out_specs=(whole, whole),
            scratch_shapes=[
                pltpu.VMEM((2, half, width), f32),
                pltpu.VMEM((2, rows, shard, width), f32),
                pltpu.VMEM((rows, shard, width), f32),
                pltpu.VMEM((2, rows, shard, width), f32),
                pltpu.VMEM((2, width, width), f32),
                pltpu.VMEM((2, extended, width), f32),
                pltpu.VMEM((extended, width), f32),
                pltpu.VMEM((extended, width), f32),
                pltpu.VMEM((2, extended, width), f32),
                pltpu.VMEM((extended, width), f32),
                pltpu.VMEM((extended, width), f32),
                pltpu.VMEM((half, width), f32),
                pltpu.VMEM((half, width), f32),
                pltpu.VMEM((2, head, width), f32),
                pltpu.VMEM((2, head, width), f32),
                pltpu.VMEM((2, head, width), f32),
                pltpu.VMEM((7, width, width), bf16),
                pltpu.VMEM((7, width, width), bf16),
                pltpu.VMEM((half, width), f32),
                pltpu.VMEM((groups, STEP, width), f32),
                pltpu.VMEM(tail_cols.shape, f32),
                dma((2, depth - 1)),
                dma((2, depth - 1)),
                dma((2, depth)),
                dma((2, depth)),
                dma((rows - 1,)),
                dma((rows - 1,)),
                dma((8,)),
                dma((8,)),
                dma((6,)),
                dma((n_all,)),
                dma((n_all,)),
                dma((n_all,)),
                dma((n_all,)),
                dma((n_data,)),
                dma((n_data,)),
                dma((n_data,)),
                dma((n_data,)),
                dma((n_data,)),
                dma((groups,)),
            ],
            compiler_params=pltpu.CompilerParams(
                collective_id=0, has_side_effects=True, vmem_limit_bytes=48 << 20
            ),
        )(*operands)

    placed = (
        P("row", "panel"),
        P("row", None),
        P(("panel", "row"), None),
        P(("panel", "row"), None),
        P(("panel", "row"), None),
        P(("row", "panel"), None),
    )
    return jax.shard_map(
        on_device,
        mesh=mesh,
        in_specs=placed,
        out_specs=(P("row", "panel"), P(("row", "panel"), None)),
        check_vma=False,
    )
```

time: 102 us -> 86.6 us (0.85)
  Pallas kernels: 99.6 us -> 84.2 us
    pallas_call x1, Pallas kernels: 99.6 us -> 84.2 us  [on_device(): pl.pallas_call(functools.partial(kernel, panels, rows), out_shape=(jax.Sh...]
where the time goes in v3:
time: 86.6 us; the launch traced here: 86.5 us
  Pallas kernels  84.2 us (97%)
  local copies, waits for them, and re-layouts  1.59 us (2%)
    pallas_call x1, Pallas kernels, on_device(): pl.pallas_call(functools.partial(kernel, panels, rows), out_shape=(jax.Sh...  84.2 us

profile of v3, /device:TPU:57, one launch (start us, length us, event | category | flops | bytes accessed | tf_op | source)
XLA Modules:
  0.0 86.5 jit_solution(16403945792429493691)
XLA Ops:
  0.6 84.2 %shard_map.77 = (f32[1024,256]{1,0:T(8,128)S(1)}, f32[32,256]{1,0:T(8,128)S(1)}) custom-call(f32[1024,256]{1,0:T(8,128)} %slab.1, f32[1024,256]{1,0:T(8,128)} %boundary.1, f32[16,256]{1,0:T(8,128)} %inverse_ref.1, f32[16,256]{1,0:T(8,128)} %beneath_ref.1, f32[16,256]{1,0:T(8,128)} %coupling_ref.1, f32[32,256]{1,0:T(8,128)} %cols_ref.1), custom_call_target="tpu_custom_call" | custom-call | tf_op jit(solution)/shard_map/pallas_call | solution.py:506
  84.9 1.0 %copy.10 = f32[1024,256]{1,0:T(8,128)} copy(f32[1024,256]{1,0:T(8,128)S(1)} %get-tuple-element.4) | data formatting | bytes 2097152
  85.8 0.6 copy.11

commit v4 on v3

--- a/solution.py
+++ b/solution.py
@@ -103,10 +103,6 @@
     def _():
         greet(ahead)
 
-    @pl.when(carried & (spot == GROUP - 2))
-    def _():
-        greet(after)
-
     @pl.when(final & carried)
     def _():
         greet(skip_ahead)
@@ -117,7 +113,7 @@
             greet(at(start + side))
 
     expected = (
-        rows + jnp.where(chip < chips - 1, 1, 0) + jnp.where(carried & final, 1, 0) + jnp.where(feeds, 1, 0)
+        rows + jnp.where(chip < chips - 1, 1, 0) + jnp.where(feeds, 1, 0)
         + jnp.where(final, jnp.where(side == core, n_data - 1, n_data), 0)
     )
     pl.semaphore_wait(barrier, expected)
@@ -163,8 +159,6 @@
             z_copy(k, i, shift, r).start()
         if k == 0:
             pair_slab.start()
-    for shift in range(1, rows):
-        g_copy(shift, r).start()
     for copy in local_shards:
         copy.wait()
 
@@ -207,6 +201,8 @@
 
     relay(0)
     relay(1)
+    for shift in range(1, rows):
+        g_copy(shift, r).start()
     x_arrivals(0)
     pair_inverse.start()
     x_arrivals(1)
@@ -244,10 +240,7 @@
     def lead_copy(b):
         return remote(passed.at[batch(b)], inflow.at[batch(b)], lead_send.at[b], in_recv.at[b], after)
 
-    def back_copy(b):
-        return remote(inflow.at[batch(b)], inflow.at[batch(b)], relay_send.at[b], in_recv.at[b], ahead)
-
-    def forth_copy(b):
+    def relay_copy(b):
         return remote(inflow.at[batch(b)], inflow.at[batch(b)], relay_send.at[b], in_recv.at[b], after)
 
     def u_copy(b):
@@ -257,9 +250,10 @@
 
     begin = jnp.where(carried, 0, n_head)
     couple_turn = n_all - 4
-    inflow_lag = jnp.where(final, 7 * group, 2 * n_all)
-    sum_lag = jnp.where(feeds & carried, inflow_lag + n_data, n_all)
-    share_lag = sum_lag + n_head + 4
+    relays = carried & (spot < GROUP - 2)
+    inflow_lag = jnp.where(final, 4 + 8 * group, 2 * n_all)
+    sum_lag = n_all
+    share_lag = jnp.maximum(sum_lag + 8, inflow_lag + 1)
     turns = 2 * n_all + n_data
 
     def turn(i, unused):
@@ -337,17 +331,13 @@
 
         m = i - inflow_lag
 
-        @pl.when(carried & (first | final) & (m >= 0) & (m < n_data))
+        @pl.when((relays | (carried & final)) & (m >= 0) & (m < n_data))
         def _():
             in_copy(m).wait_recv()
 
-            @pl.when(first)
-            def _():
-                forth_copy(m).start()
-
-            @pl.when(final & jnp.logical_not(feeds))
-            def _():
-                back_copy(m).start()
+            @pl.when(relays)
+            def _():
+                relay_copy(m).start()
 
             @pl.when(final)
             def _():
@@ -357,14 +347,6 @@
             def _():
                 in_copy(m).start()
                 lead_copy(m).start()
-
-        @pl.when(carried & feeds & (m == n_data))
-        def _():
-            def hand_back(k, unused):
-                back_copy(k).start()
-                return unused
-
-            lax.fori_loop(0, n_data, hand_back, 0)
 
         @pl.when(carried & final & (i == share_lag))
         def _():
@@ -408,7 +390,7 @@
 
         lax.fori_loop(begin, n_all, sent, 0)
 
-    @pl.when(carried & (spot > 0) & (spot < GROUP - 1))
+    @pl.when(carried & (spot == GROUP - 2))
     def _():
         def reached(b, unused):
             in_copy(b).wait_recv()
@@ -448,9 +430,9 @@
             in_copy(b).wait_send()
             lead_copy(b).wait_send()
 
-        @pl.when(carried & (first | final))
-        def _():
-            back_copy(b).wait_send()
+        @pl.when(relays)
+        def _():
+            relay_copy(b).wait_send()
 
         @pl.when(final & (core * n_data + b != p))
         def _():

time: 86.6 us -> 80.1 us (0.925)
  Pallas kernels: 84.2 us -> 77.1 us
    pallas_call x1, Pallas kernels: 84.2 us -> 77.1 us  [on_device(): pl.pallas_call(functools.partial(kernel, panels, rows), out_shape=(jax.Sh...]
where the time goes in v4:
time: 80.1 us; the launch traced here: 79.3 us
  Pallas kernels  77.1 us (96%)
  local copies, waits for them, and re-layouts  1.59 us (2%)
    pallas_call x1, Pallas kernels, on_device(): pl.pallas_call(functools.partial(kernel, panels, rows), out_shape=(jax.Sh...  77.1 us

profile of v4, /device:TPU:57, one launch (start us, length us, event | category | flops | bytes accessed | tf_op | source)
XLA Modules:
  0.0 79.3 jit_solution(15541211098344224153)
XLA Ops:
  0.6 77.1 %shard_map.77 = (f32[1024,256]{1,0:T(8,128)S(1)}, f32[32,256]{1,0:T(8,128)S(1)}) custom-call(f32[1024,256]{1,0:T(8,128)} %slab.1, f32[1024,256]{1,0:T(8,128)} %boundary.1, f32[16,256]{1,0:T(8,128)} %inverse_ref.1, f32[16,256]{1,0:T(8,128)} %beneath_ref.1, f32[16,256]{1,0:T(8,128)} %coupling_ref.1, f32[32,256]{1,0:T(8,128)} %cols_ref.1), custom_call_target="tpu_custom_call" | custom-call | tf_op jit(solution)/shard_map/pallas_call | solution.py:488
  77.7 1.0 %copy.10 = f32[1024,256]{1,0:T(8,128)} copy(f32[1024,256]{1,0:T(8,128)S(1)} %get-tuple-element.4) | data formatting | bytes 2097152
  78.7 0.6 copy.11

commit v5 on v4

--- a/solution.py
+++ b/solution.py
@@ -32,8 +32,8 @@
     slab, boundary, inverse_ref, beneath_ref, coupling_ref, cols_ref,
     factor_ref, tail_ref,
     slabs, inverses, beneath, couplings, products, constants, offset, entering, solved,
-    sums_in, sums_out, inflow, passed, carry, carry_even, carry_sum, weight_high, weight_low, share, total, cols,
-    z_send, z_recv, x_send, x_recv, g_send, g_recv, pair_send, pair_recv, local_sem,
+    sums_in, sums_out, inflow, passed, carry, carry_even, carry_sum, fixed, weight_high, weight_low, share, total, cols,
+    z_send, z_recv, x_send, x_recv, g_send, g_recv, k_send, k_recv, f_send, f_recv, pair_send, pair_recv, local_sem,
     y_send, y_recv, t_send, t_recv, in_send, in_recv, lead_send, relay_send, u_send, u_recv,
 ):
     p, r = lax.axis_index("panel"), lax.axis_index("row")
@@ -50,10 +50,12 @@
     head = width // 2
     n_head, n_data = head // STEP, half // STEP
     n_all = n_head + n_data
+    n_sum = 1 + n_data
+    piece = head // rows
     body = pl.ds(head, half)
     mine = pl.ds(pl.multiple_of(core * half, half), half)
     other = pl.ds(pl.multiple_of((1 - core) * half, half), half)
-    steps = sorted(range(1, depth), key=lambda d: (min(d, depth - d), d))
+    steps = sorted(range(1, depth), key=lambda d: (-min(d, depth - d), d))
 
     first, final = spot == 0, spot == GROUP - 1
     carried = group > 0
@@ -150,8 +152,7 @@
     pair_coupling = to_sibling(3, couplings.at[core], couplings.at[core])
     pair_carry = to_sibling(4, solved.at[1, pl.ds(0, head)], carry.at[core])
     pair_even = to_sibling(5, solved.at[0, pl.ds(0, head)], carry_even.at[core])
-    pair_sum = to_sibling(6, sums_out.at[pl.ds(0, head)], carry_sum.at[core])
-    pair_factor = to_sibling(7, solved.at[1 - core, body], factor_ref.at[mine])
+    pair_sum = to_sibling(6, carry_sum.at[core], carry_sum.at[core])
 
     for k in range(2):
         x_own(k).start()
@@ -231,8 +232,26 @@
     def y_copy(b):
         return remote(solved.at[1, batch(b)], entering.at[batch(b)], y_send.at[b], y_recv.at[b], after)
 
-    def t_copy(b):
-        return remote(sums_out.at[batch(b)], sums_in.at[batch(b)], t_send.at[b], t_recv.at[b], after)
+    def part_of(row):
+        return pl.ds(pl.multiple_of(row * piece, piece), piece)
+
+    def t_copy(b, place):
+        return remote(sums_out.at[place], sums_in.at[place], t_send.at[b], t_recv.at[b], after)
+
+    def k_copy(shift, place):
+        return remote(
+            sums_out.at[part_of(r)], carry_sum.at[core, place], k_send.at[shift - 1], k_recv.at[shift - 1],
+            {"panel": p, "row": any_row(shift)},
+        )
+
+    def factor_copy(b):
+        place = pl.ds(pl.multiple_of(core * half + b * STEP, STEP), STEP)
+        return remote(solved.at[1 - core, data(b)], factor_ref.at[place], f_send.at[b], f_recv.at[b], sibling)
+
+    def hand_in(b):
+        place = pl.ds(pl.multiple_of(core * half + b * STEP, STEP), STEP)
+        factor_copy(b).start()
+        factor_ref[place] = solved[core, data(b)]
 
     def in_copy(b):
         return remote(passed.at[batch(b)], inflow.at[batch(b)], in_send.at[b], in_recv.at[b], skip_after)
@@ -249,12 +268,14 @@
         )
 
     begin = jnp.where(carried, 0, n_head)
-    couple_turn = n_all - 4
+    couple_turn = jnp.where(final, 8, n_all - 4)
+    fix_turn = jnp.where(final, 12, n_all)
     relays = carried & (spot < GROUP - 2)
-    inflow_lag = jnp.where(final, 4 + 8 * group, 2 * n_all)
+    fills = carried & (spot < GROUP - 1)
+    inflow_lag = jnp.where(final, 8 * group, n_all + n_sum + 1)
     sum_lag = n_all
-    share_lag = jnp.maximum(sum_lag + 8, inflow_lag + 1)
-    turns = 2 * n_all + n_data
+    share_lag = jnp.where(carried, sum_lag + 13, sum_lag + 2)
+    turns = n_all + n_sum + 1 + n_data
 
     def turn(i, unused):
         @pl.when((i >= begin) & (i < n_all))
@@ -287,57 +308,99 @@
                 g_copy(shift, any_row(-shift)).wait_recv()
             pair_coupling.start()
 
-        @pl.when(i == sum_lag)
+        @pl.when(i == fix_turn)
         def _():
             pair_coupling.wait_recv()
             keep(2, square(couplings.at[0]))
             keep(3, square(couplings.at[1]))
 
+        @pl.when(final & (i == fix_turn))
+        def _():
+            step = weight_high[0].astype(jnp.float32) + weight_low[0].astype(jnp.float32)
+            keep(7, times(step, 3) - times(products[0].T, 2))
+            fixed[...] = times(constants[0, body], 2) + times(offset[body], 3)
+
         b = i - sum_lag
 
-        @pl.when((b >= begin) & (b < n_all))
-        def _():
-            even = constants[0, batch(b)] - times(entering[batch(b)], 1)
-            solved[0, batch(b)] = even
-            part = times(even, 2) + times(solved[1, batch(b)], 3)
-
+        def add_up(place, part):
             @pl.when(first)
             def _():
-                sums_out[batch(b)] = part
+                sums_out[place] = part
 
             @pl.when(spot > 0)
             def _():
-                t_copy(b).wait_recv()
-                sums_out[batch(b)] = sums_in[batch(b)] + part
+                t_copy(b, place).wait_recv()
+                sums_out[place] = sums_in[place] + part
 
             @pl.when(spot < GROUP - 1)
             def _():
-                t_copy(b).start()
-
-        @pl.when(carried & (b == n_head))
-        def _():
+                t_copy(b, place).start()
+
+        @pl.when(carried & (b == 0))
+        def _():
+            place = part_of(r)
+            solved[0, :head] = -times(entering[:head], 1)
+            add_up(place, times(solved[0, place], 2) + times(solved[1, place], 3))
             pair_even.start()
             carry_even[core] = solved[0, :head]
 
-        @pl.when(carried & final & (b == n_head))
-        def _():
+        @pl.when((b > 0) & (b < n_sum) & (spot < GROUP - 1))
+        def _():
+            place = data(b - 1)
+            even = constants[0, place] - times(entering[place], 1)
+            solved[0, place] = even
+            add_up(place, times(even, 2) + times(solved[1, place], 3))
+
+        @pl.when((b > 0) & (b < n_sum) & final)
+        def _():
+            place = data(b - 1)
+            add_up(place, fixed[batch(b - 1)] + times(entering[place], 7))
+
+        @pl.when(carried & final & (b == 0))
+        def _():
+            carry_sum[core, part_of(r)] = sums_out[part_of(r)]
+            for shift in range(1, rows):
+                k_copy(shift, part_of(r)).start()
+
+        @pl.when(carried & final & (i == share_lag - 3))
+        def _():
+            for shift in range(1, rows):
+                k_copy(shift, part_of(any_row(-shift))).wait_recv()
             pair_sum.start()
-            carry_sum[core] = sums_out[:head]
-
-        @pl.when(carried & final & (i == inflow_lag))
-        def _():
+
+        @pl.when(fills & (i == inflow_lag))
+        def _():
+            def sent(k, unused):
+                y_copy(k).wait_send()
+                return unused
+
+            lax.fori_loop(begin, n_all, sent, 0)
             pair_carry.wait_recv()
             keep(4, carry[...].reshape(width, width))
+            pair_even.wait_recv()
+            keep(5, carry_even[...].reshape(width, width))
+
+        @pl.when(carried & final & (i == inflow_lag))
+        def _():
+            pair_carry.wait_recv()
+            keep(4, carry[...].reshape(width, width))
 
         m = i - inflow_lag
 
-        @pl.when((relays | (carried & final)) & (m >= 0) & (m < n_data))
+        @pl.when(carried & (m >= 0) & (m < n_data))
         def _():
             in_copy(m).wait_recv()
 
             @pl.when(relays)
             def _():
                 relay_copy(m).start()
+
+            @pl.when(spot < GROUP - 1)
+            def _():
+                value = inflow[batch(m)]
+                solved[1, data(m)] += times(value, 4)
+                solved[0, data(m)] += times(value, 5)
+                hand_in(m)
 
             @pl.when(final)
             def _():
@@ -383,35 +446,41 @@
 
     @pl.when(spot < GROUP - 1)
     def _():
-        def sent(b, unused):
-            y_copy(b).wait_send()
-            t_copy(b).wait_send()
+        @pl.when(group == 0)
+        def _():
+            def sent(k, unused):
+                y_copy(k).wait_send()
+                return unused
+
+            lax.fori_loop(begin, n_all, sent, 0)
+
+        @pl.when(carried)
+        def _():
+            t_copy(0, part_of(r)).wait_send()
+
+        def summed_up(k, unused):
+            t_copy(k, data(k - 1)).wait_send()
             return unused
 
-        lax.fori_loop(begin, n_all, sent, 0)
-
-    @pl.when(carried & (spot == GROUP - 2))
-    def _():
-        def reached(b, unused):
-            in_copy(b).wait_recv()
-            return unused
-
-        lax.fori_loop(0, n_data, reached, 0)
-
-    @pl.when(carried & (spot < GROUP - 1))
-    def _():
-        pair_carry.wait_recv()
-        keep(4, carry[...].reshape(width, width))
-        solved[1, body] += times(inflow[...], 4)
-
-    @pl.when(carried)
+        lax.fori_loop(1, n_sum, summed_up, 0)
+
+    @pl.when(final)
+    def _():
+        solved[0, body] = constants[0, body] - times(entering[body], 1)
+
+    @pl.when(final & carried)
     def _():
         pair_even.wait_recv()
         keep(5, carry_even[...].reshape(width, width))
         solved[0, body] += times(inflow[...], 5)
 
-    pair_factor.start()
-    factor_ref[mine] = solved[core, body]
+    @pl.when(jnp.logical_not(fills))
+    def _():
+        def hand_all(k, unused):
+            hand_in(k)
+            return unused
+
+        lax.fori_loop(0, n_data, hand_all, 0)
 
     for k, start in enumerate(source_panels):
         @pl.when(start + side != p)
@@ -425,6 +494,8 @@
     tail_ref[...] = cols[...] - summed
 
     def drain(b, unused):
+        factor_copy(b).wait()
+
         @pl.when(feeds)
         def _():
             in_copy(b).wait_send()
@@ -462,8 +533,8 @@
     @pl.when(carried & final)
     def _():
         pair_sum.wait_send()
-
-    pair_factor.wait()
+        for shift in range(1, rows):
+            k_copy(shift, part_of(r)).wait_send()
 
 
 def solution(mesh):
@@ -510,8 +581,9 @@
                 pltpu.VMEM((2, head, width), f32),
                 pltpu.VMEM((2, head, width), f32),
                 pltpu.VMEM((2, head, width), f32),
-                pltpu.VMEM((7, width, width), bf16),
-                pltpu.VMEM((7, width, width), bf16),
+                pltpu.VMEM((half, width), f32),
+                pltpu.VMEM((8, width, width), bf16),
+                pltpu.VMEM((8, width, width), bf16),
                 pltpu.VMEM((half, width), f32),
                 pltpu.VMEM((groups, STEP, width), f32),
                 pltpu.VMEM(tail_cols.shape, f32),
@@ -521,8 +593,12 @@
                 dma((2, depth)),
                 dma((rows - 1,)),
                 dma((rows - 1,)),
-                dma((8,)),
-                dma((8,)),
+                dma((rows - 1,)),
+                dma((rows - 1,)),
+                dma((n_data,)),
+                dma((n_data,)),
+                dma((7,)),
+                dma((7,)),
                 dma((6,)),
                 dma((n_all,)),
                 dma((n_all,)),

time: 80.1 us -> 78.6 us (0.981)
  Pallas kernels: 77.1 us -> 76.2 us
    pallas_call x1, Pallas kernels: 77.1 us -> 76.2 us  [on_device(): pl.pallas_call(functools.partial(kernel, panels, rows), out_shape=(jax.Sh...]
where the time goes in v5:
time: 78.6 us; the launch traced here: 78.4 us
  Pallas kernels  76.2 us (97%)
  local copies, waits for them, and re-layouts  1.59 us (2%)
    pallas_call x1, Pallas kernels, on_device(): pl.pallas_call(functools.partial(kernel, panels, rows), out_shape=(jax.Sh...  76.2 us
    unnamed x2, local copies, waits for them, and re-layouts  1.59 us

profile of v5, /device:TPU:57, one launch (start us, length us, event | category | flops | bytes accessed | tf_op | source)
XLA Modules:
  0.0 78.4 jit_solution(17299288553273923013)
XLA Ops:
  0.6 76.2 %shard_map.77 = (f32[1024,256]{1,0:T(8,128)S(1)}, f32[32,256]{1,0:T(8,128)S(1)}) custom-call(f32[1024,256]{1,0:T(8,128)} %slab.1, f32[1024,256]{1,0:T(8,128)} %boundary.1, f32[16,256]{1,0:T(8,128)} %inverse_ref.1, f32[16,256]{1,0:T(8,128)} %beneath_ref.1, f32[16,256]{1,0:T(8,128)} %coupling_ref.1, f32[32,256]{1,0:T(8,128)} %cols_ref.1), custom_call_target="tpu_custom_call" | custom-call | tf_op jit(solution)/shard_map/pallas_call | solution.py:559
  76.9 1.0 %copy.10 = f32[1024,256]{1,0:T(8,128)} copy(f32[1024,256]{1,0:T(8,128)S(1)} %get-tuple-element.4) | data formatting | bytes 2097152
  77.8 0.6 copy.11

commit v6 on v5

--- a/solution.py
+++ b/solution.py
@@ -127,19 +127,19 @@
 
     def z_copy(k, i, shift, place):
         return remote(
-            shards[k], full[k].at[place], z_send.at[k, i], z_recv.at[k, i], {"panel": p, "row": z_row(shift)}
+            shards[k], full[k].at[place], z_send.at[0], z_recv.at[k, i], {"panel": p, "row": z_row(shift)}
         )
 
     def x_own(k):
-        return remote(shards[k], full[k].at[r], x_send.at[k, depth - 1], x_recv.at[k, depth - 1], beside)
+        return remote(shards[k], full[k].at[r], x_send.at[0], x_recv.at[k], beside)
 
     def x_relay(k, i, shift):
         place = full[k].at[z_row(-shift)]
-        return remote(place, place, x_send.at[k, i], x_recv.at[k, i], beside)
+        return remote(place, place, x_send.at[0], x_recv.at[k], beside)
 
     def g_copy(shift, place):
         return remote(
-            shards[2], full[2].at[place], g_send.at[shift - 1], g_recv.at[shift - 1],
+            shards[2], full[2].at[place], g_send.at[0], g_recv.at[0],
             {"panel": p, "row": any_row(shift)},
         )
 
@@ -168,10 +168,14 @@
             z_copy(k, i, shift, z_row(-shift)).wait_recv()
             x_relay(k, i, shift).start()
 
+    def sent(ref, sem):
+        remote(ref, ref, sem.at[0], sem.at[0], sibling).wait_send()
+
+    def received(ref, sem):
+        remote(ref, ref, sem, sem, sibling).wait_recv()
+
     def x_arrivals(k):
-        x_own(k).wait_recv()
-        for i, shift in enumerate(steps):
-            x_relay(k, i, shift).wait_recv()
+        received(full[k].at[pl.ds(0, depth)], x_recv.at[k])
 
     def square(ref):
         return ref[...].reshape(width, width)
@@ -230,23 +234,23 @@
         return pl.ds(pl.multiple_of(b * STEP + head, STEP), STEP)
 
     def y_copy(b):
-        return remote(solved.at[1, batch(b)], entering.at[batch(b)], y_send.at[b], y_recv.at[b], after)
+        return remote(solved.at[1, batch(b)], entering.at[batch(b)], y_send.at[0], y_recv.at[b], after)
 
     def part_of(row):
         return pl.ds(pl.multiple_of(row * piece, piece), piece)
 
     def t_copy(b, place):
-        return remote(sums_out.at[place], sums_in.at[place], t_send.at[b], t_recv.at[b], after)
+        return remote(sums_out.at[place], sums_in.at[place], t_send.at[0], t_recv.at[b], after)
 
     def k_copy(shift, place):
         return remote(
-            sums_out.at[part_of(r)], carry_sum.at[core, place], k_send.at[shift - 1], k_recv.at[shift - 1],
+            sums_out.at[part_of(r)], carry_sum.at[core, place], k_send.at[0], k_recv.at[0],
             {"panel": p, "row": any_row(shift)},
         )
 
     def factor_copy(b):
         place = pl.ds(pl.multiple_of(core * half + b * STEP, STEP), STEP)
-        return remote(solved.at[1 - core, data(b)], factor_ref.at[place], f_send.at[b], f_recv.at[b], sibling)
+        return remote(solved.at[1 - core, data(b)], factor_ref.at[place], f_send.at[0], f_recv.at[0], sibling)
 
     def hand_in(b):
         place = pl.ds(pl.multiple_of(core * half + b * STEP, STEP), STEP)
@@ -254,17 +258,17 @@
         factor_ref[place] = solved[core, data(b)]
 
     def in_copy(b):
-        return remote(passed.at[batch(b)], inflow.at[batch(b)], in_send.at[b], in_recv.at[b], skip_after)
+        return remote(passed.at[batch(b)], inflow.at[batch(b)], in_send.at[0], in_recv.at[b], skip_after)
 
     def lead_copy(b):
-        return remote(passed.at[batch(b)], inflow.at[batch(b)], lead_send.at[b], in_recv.at[b], after)
+        return remote(passed.at[batch(b)], inflow.at[batch(b)], lead_send.at[0], in_recv.at[b], after)
 
     def relay_copy(b):
-        return remote(inflow.at[batch(b)], inflow.at[batch(b)], relay_send.at[b], in_recv.at[b], after)
+        return remote(inflow.at[batch(b)], inflow.at[batch(b)], relay_send.at[0], in_recv.at[b], after)
 
     def u_copy(b):
         return remote(
-            share.at[batch(b)], total.at[group], u_send.at[b], u_recv.at[group], at(core * n_data + b)
+            share.at[batch(b)], total.at[group], u_send.at[0], u_recv.at[group], at(core * n_data + b)
         )
 
     begin = jnp.where(carried, 0, n_head)
@@ -274,7 +278,7 @@
     fills = carried & (spot < GROUP - 1)
     inflow_lag = jnp.where(final, 8 * group, n_all + n_sum + 1)
     sum_lag = n_all
-    share_lag = jnp.where(carried, sum_lag + 13, sum_lag + 2)
+    share_lag = jnp.where(carried, sum_lag + 13, sum_lag + 9)
     turns = n_all + n_sum + 1 + n_data
 
     def turn(i, unused):
@@ -304,8 +308,7 @@
 
         @pl.when(i == couple_turn)
         def _():
-            for shift in range(1, rows):
-                g_copy(shift, any_row(-shift)).wait_recv()
+            received(couplings.at[core, pl.ds(0, rows - 1)], g_recv.at[0])
             pair_coupling.start()
 
         @pl.when(i == fix_turn)
@@ -364,17 +367,12 @@
 
         @pl.when(carried & final & (i == share_lag - 3))
         def _():
-            for shift in range(1, rows):
-                k_copy(shift, part_of(any_row(-shift))).wait_recv()
+            received(carry_sum.at[core, pl.ds(0, (rows - 1) * piece)], k_recv.at[0])
             pair_sum.start()
 
         @pl.when(fills & (i == inflow_lag))
         def _():
-            def sent(k, unused):
-                y_copy(k).wait_send()
-                return unused
-
-            lax.fori_loop(begin, n_all, sent, 0)
+            sent(entering, y_send)
             pair_carry.wait_recv()
             keep(4, carry[...].reshape(width, width))
             pair_even.wait_recv()
@@ -418,23 +416,27 @@
 
         t = i - share_lag
 
-        @pl.when(final & (t >= 0) & (t < n_data))
-        def _():
+        @pl.when(final & (t >= 0) & (t < n_data // 2))
+        def _():
+            pair = pl.ds(pl.multiple_of(t * 2 * STEP, 2 * STEP), 2 * STEP)
+            below = pl.ds(pl.multiple_of(t * 2 * STEP + head, 2 * STEP), 2 * STEP)
+
             @pl.when(carried)
             def _():
-                share[batch(t)] = sums_out[data(t)] + times(inflow[batch(t)], 6)
+                share[pair] = sums_out[below] + times(inflow[pair], 6)
 
             @pl.when(group == 0)
             def _():
-                share[batch(t)] = sums_out[data(t)]
-
-            @pl.when(core * n_data + t != p)
-            def _():
-                u_copy(t).start()
-
-            @pl.when(core * n_data + t == p)
-            def _():
-                total[group] = share[batch(t)]
+                share[pair] = sums_out[below]
+
+            for b in (2 * t, 2 * t + 1):
+                @pl.when(core * n_data + b != p)
+                def _():
+                    u_copy(b).start()
+
+                @pl.when(core * n_data + b == p)
+                def _():
+                    total[group] = share[batch(b)]
 
         return unused
 
@@ -448,21 +450,12 @@
     def _():
         @pl.when(group == 0)
         def _():
-            def sent(k, unused):
-                y_copy(k).wait_send()
-                return unused
-
-            lax.fori_loop(begin, n_all, sent, 0)
+            sent(entering.at[body], y_send)
+            sent(sums_in.at[body], t_send)
 
         @pl.when(carried)
         def _():
-            t_copy(0, part_of(r)).wait_send()
-
-        def summed_up(k, unused):
-            t_copy(k, data(k - 1)).wait_send()
-            return unused
-
-        lax.fori_loop(1, n_sum, summed_up, 0)
+            sent(sums_in.at[pl.ds(0, piece + half)], t_send)
 
     @pl.when(final)
     def _():
@@ -493,33 +486,29 @@
         summed = summed + total[k]
     tail_ref[...] = cols[...] - summed
 
-    def drain(b, unused):
-        factor_copy(b).wait()
-
-        @pl.when(feeds)
-        def _():
-            in_copy(b).wait_send()
-            lead_copy(b).wait_send()
-
-        @pl.when(relays)
-        def _():
-            relay_copy(b).wait_send()
-
-        @pl.when(final & (core * n_data + b != p))
-        def _():
-            u_copy(b).wait_send()
-
-        return unused
-
-    lax.fori_loop(0, n_data, drain, 0)
-
-    for k in range(2):
-        x_own(k).wait_send()
-        for i, shift in enumerate(steps):
-            z_copy(k, i, shift, r).wait_send()
-            x_relay(k, i, shift).wait_send()
-    for shift in range(1, rows):
-        g_copy(shift, r).wait_send()
+    received(factor_ref.at[mine], f_recv.at[0])
+    sent(factor_ref.at[mine], f_send)
+
+    @pl.when(feeds)
+    def _():
+        sent(inflow, in_send)
+        sent(inflow, lead_send)
+
+    @pl.when(relays)
+    def _():
+        sent(inflow, relay_send)
+
+    @pl.when(final & (side == core))
+    def _():
+        sent(share.at[pl.ds(0, half - STEP)], u_send)
+
+    @pl.when(final & (side != core))
+    def _():
+        sent(share, u_send)
+
+    sent(inverses.at[core, pl.ds(0, 2 * depth - 2)], z_send)
+    sent(inverses.at[core], x_send)
+    sent(couplings.at[core, pl.ds(0, rows - 1)], g_send)
     pair_slab.wait_send()
     pair_inverse.wait_send()
     pair_product.wait_send()
@@ -533,8 +522,7 @@
     @pl.when(carried & final)
     def _():
         pair_sum.wait_send()
-        for shift in range(1, rows):
-            k_copy(shift, part_of(r)).wait_send()
+        sent(carry_sum.at[core, pl.ds(0, (rows - 1) * piece)], k_send)
 
 
 def solution(mesh):
@@ -587,28 +575,28 @@
                 pltpu.VMEM((half, width), f32),
                 pltpu.VMEM((groups, STEP, width), f32),
                 pltpu.VMEM(tail_cols.shape, f32),
+                dma((1,)),
                 dma((2, depth - 1)),
-                dma((2, depth - 1)),
-                dma((2, depth)),
-                dma((2, depth)),
-                dma((rows - 1,)),
-                dma((rows - 1,)),
-                dma((rows - 1,)),
-                dma((rows - 1,)),
-                dma((n_data,)),
-                dma((n_data,)),
+                dma((1,)),
+                dma((2,)),
+                dma((1,)),
+                dma((1,)),
+                dma((1,)),
+                dma((1,)),
+                dma((1,)),
+                dma((1,)),
                 dma((7,)),
                 dma((7,)),
                 dma((6,)),
+                dma((1,)),
                 dma((n_all,)),
-                dma((n_all,)),
-                dma((n_all,)),
-                dma((n_all,)),
+                dma((1,)),
+                dma((n_data + 1,)),
+                dma((1,)),
                 dma((n_data,)),
-                dma((n_data,)),
-                dma((n_data,)),
-                dma((n_data,)),
-                dma((n_data,)),
+                dma((1,)),
+                dma((1,)),
+                dma((1,)),
                 dma((groups,)),
             ],
             compiler_params=pltpu.CompilerParams(

time: 78.6 us -> 75.4 us (0.959)
  Pallas kernels: 76.2 us -> 72.7 us
    pallas_call x1, Pallas kernels: 76.2 us -> 72.7 us  [on_device(): pl.pallas_call(functools.partial(kernel, panels, rows), out_shape=(jax.Sh...]
where the time goes in v6:
time: 75.4 us; the launch traced here: 75 us
  Pallas kernels  72.7 us (96%)
  local copies, waits for them, and re-layouts  1.59 us (2%)
    pallas_call x1, Pallas kernels, on_device(): pl.pallas_call(functools.partial(kernel, panels, rows), out_shape=(jax.Sh...  72.7 us
    unnamed x2, local copies, waits for them, and re-layouts  1.59 us

profile of v6, /device:TPU:57, one launch (start us, length us, event | category | flops | bytes accessed | tf_op | source)
XLA Modules:
  0.0 75.0 jit_solution(4885167321121319164)
XLA Ops:
  0.6 72.7 %shard_map.77 = (f32[1024,256]{1,0:T(8,128)S(1)}, f32[32,256]{1,0:T(8,128)S(1)}) custom-call(f32[1024,256]{1,0:T(8,128)} %slab.1, f32[1024,256]{1,0:T(8,128)} %boundary.1, f32[16,256]{1,0:T(8,128)} %inverse_ref.1, f32[16,256]{1,0:T(8,128)} %beneath_ref.1, f32[16,256]{1,0:T(8,128)} %coupling_ref.1, f32[32,256]{1,0:T(8,128)} %cols_ref.1), custom_call_target="tpu_custom_call" | custom-call | tf_op jit(solution)/shard_map/pallas_call | solution.py:547
  73.4 1.0 %copy.10 = f32[1024,256]{1,0:T(8,128)} copy(f32[1024,256]{1,0:T(8,128)S(1)} %get-tuple-element.4) | data formatting | bytes 2097152
  74.3 0.6 copy.11

commit v7 on v6

--- a/solution.py
+++ b/solution.py
@@ -34,7 +34,7 @@
     slabs, inverses, beneath, couplings, products, constants, offset, entering, solved,
     sums_in, sums_out, inflow, passed, carry, carry_even, carry_sum, fixed, weight_high, weight_low, share, total, cols,
     z_send, z_recv, x_send, x_recv, g_send, g_recv, k_send, k_recv, f_send, f_recv, pair_send, pair_recv, local_sem,
-    y_send, y_recv, t_send, t_recv, in_send, in_recv, lead_send, relay_send, u_send, u_recv,
+    y_send, y_recv, t_send, t_recv, in_send, in_recv, lead_send, relay_send, back_send, u_send, u_recv,
 ):
     p, r = lax.axis_index("panel"), lax.axis_index("row")
     core = lax.rem(p, 2)
@@ -60,6 +60,7 @@
     first, final = spot == 0, spot == GROUP - 1
     carried = group > 0
     feeds = final & (group < groups - 1)
+    halved = group == 1
 
     def at(panel):
         return {"panel": panel, "row": r}
@@ -76,6 +77,32 @@
     def any_row(shift):
         return lax.rem(r + shift + rows, rows)
 
+    barrier = pltpu.get_barrier_semaphore()
+
+    def greet(target):
+        pl.semaphore_signal(barrier, inc=1, device_id=target, device_id_type=MESH)
+
+    for shift in range(1, rows):
+        greet({"panel": p, "row": any_row(shift)})
+    greet(sibling)
+
+    @pl.when(chip > 0)
+    def _():
+        greet(ahead)
+
+    @pl.when(halved & (spot == GROUP - 2))
+    def _():
+        greet(after)
+
+    @pl.when(final & carried)
+    def _():
+        greet(skip_ahead)
+
+    for start in source_panels:
+        @pl.when(start + side != p)
+        def _():
+            greet(at(start + side))
+
     local_slab = pltpu.make_async_copy(slab.at[mine], slabs.at[core], local_sem.at[0])
     local_slab.start()
     local_cols = pltpu.make_async_copy(cols_ref, cols, local_sem.at[1])
@@ -92,30 +119,8 @@
     for copy in local_shards:
         copy.start()
 
-    barrier = pltpu.get_barrier_semaphore()
-
-    def greet(target):
-        pl.semaphore_signal(barrier, inc=1, device_id=target, device_id_type=MESH)
-
-    for shift in range(1, rows):
-        greet({"panel": p, "row": any_row(shift)})
-    greet(sibling)
-
-    @pl.when(chip > 0)
-    def _():
-        greet(ahead)
-
-    @pl.when(final & carried)
-    def _():
-        greet(skip_ahead)
-
-    for start in source_panels:
-        @pl.when(start + side != p)
-        def _():
-            greet(at(start + side))
-
     expected = (
-        rows + jnp.where(chip < chips - 1, 1, 0) + jnp.where(feeds, 1, 0)
+        rows + jnp.where(chip < chips - 1, 1, 0) + jnp.where(feeds, 1, 0) + jnp.where(halved & final, 1, 0)
         + jnp.where(final, jnp.where(side == core, n_data - 1, n_data), 0)
     )
     pl.semaphore_wait(barrier, expected)
@@ -206,18 +211,18 @@
 
     relay(0)
     relay(1)
-    for shift in range(1, rows):
-        g_copy(shift, r).start()
     x_arrivals(0)
     pair_inverse.start()
-    x_arrivals(1)
-    products[core] = dot3(square(inverses.at[core]), square(beneath), NN)
-    pair_product.start()
     local_slab.wait()
     constants[core, body] = dot3(slabs[core], square(inverses.at[core]), NT)
     pair_slab.wait_recv()
     pair_inverse.wait_recv()
     constants[1 - core, body] = dot3(slabs[1 - core], square(inverses.at[1 - core]), NT)
+    x_arrivals(1)
+    products[core] = dot3(square(inverses.at[core]), square(beneath), NN)
+    pair_product.start()
+    for shift in range(1, rows):
+        g_copy(shift, r).start()
     pair_product.wait_recv()
     keep(0, dot3(products[1], products[0], NN).T)
     offset[body] = constants[1, body] - dot3(constants[0, body], products[1], NT)
@@ -265,6 +270,9 @@
 
     def relay_copy(b):
         return remote(inflow.at[batch(b)], inflow.at[batch(b)], relay_send.at[0], in_recv.at[b], after)
+
+    def back_copy(b):
+        return remote(inflow.at[batch(b)], inflow.at[batch(b)], back_send.at[0], in_recv.at[b], ahead)
 
     def u_copy(b):
         return remote(
@@ -389,9 +397,13 @@
         def _():
             in_copy(m).wait_recv()
 
-            @pl.when(relays)
+            @pl.when(relays & (first | jnp.logical_not(halved) | (m < n_data // 2)))
             def _():
                 relay_copy(m).start()
+
+            @pl.when(final & halved & jnp.logical_not(feeds) & (m >= n_data // 2))
+            def _():
+                back_copy(m).start()
 
             @pl.when(spot < GROUP - 1)
             def _():
@@ -408,6 +420,14 @@
             def _():
                 in_copy(m).start()
                 lead_copy(m).start()
+
+        @pl.when(feeds & halved & (m == n_data))
+        def _():
+            def give_back(k, unused):
+                back_copy(k).start()
+                return unused
+
+            lax.fori_loop(n_data // 2, n_data, give_back, 0)
 
         @pl.when(carried & final & (i == share_lag))
         def _():
@@ -494,9 +514,19 @@
         sent(inflow, in_send)
         sent(inflow, lead_send)
 
-    @pl.when(relays)
+    part_relay = relays & halved & (spot > 0)
+
+    @pl.when(relays & jnp.logical_not(part_relay))
     def _():
         sent(inflow, relay_send)
+
+    @pl.when(part_relay)
+    def _():
+        sent(inflow.at[pl.ds(0, half // 2)], relay_send)
+
+    @pl.when(halved & final)
+    def _():
+        sent(inflow.at[pl.ds(0, half // 2)], back_send)
 
     @pl.when(final & (side == core))
     def _():
@@ -597,6 +627,7 @@
                 dma((1,)),
                 dma((1,)),
                 dma((1,)),
+                dma((1,)),
                 dma((groups,)),
             ],
             compiler_params=pltpu.CompilerParams(

time: 75.4 us -> 74.8 us (level)
    pallas_call x1, Pallas kernels: 72.7 us -> 72 us  [on_device(): pl.pallas_call(functools.partial(kernel, panels, rows), out_shape=(jax.Sh...]
where the time goes in v7:
time: 74.8 us; the launch traced here: 74.2 us
  Pallas kernels  72 us (96%)
  local copies, waits for them, and re-layouts  1.59 us (2%)
    pallas_call x1, Pallas kernels, on_device(): pl.pallas_call(functools.partial(kernel, panels, rows), out_shape=(jax.Sh...  72 us
    unnamed x2, local copies, waits for them, and re-layouts  1.59 us

profile of v7, /device:TPU:57, one launch (start us, length us, event | category | flops | bytes accessed | tf_op | source)
XLA Modules:
  0.0 74.2 jit_solution(16714119677566694368)
XLA Ops:
  0.6 72.0 %shard_map.77 = (f32[1024,256]{1,0:T(8,128)S(1)}, f32[32,256]{1,0:T(8,128)S(1)}) custom-call(f32[1024,256]{1,0:T(8,128)} %slab.1, f32[1024,256]{1,0:T(8,128)} %boundary.1, f32[16,256]{1,0:T(8,128)} %inverse_ref.1, f32[16,256]{1,0:T(8,128)} %beneath_ref.1, f32[16,256]{1,0:T(8,128)} %coupling_ref.1, f32[32,256]{1,0:T(8,128)} %cols_ref.1), custom_call_target="tpu_custom_call" | custom-call | tf_op jit(solution)/shard_map/pallas_call | solution.py:577
  72.6 1.0 %copy.10 = f32[1024,256]{1,0:T(8,128)} copy(f32[1024,256]{1,0:T(8,128)S(1)} %get-tuple-element.4) | data formatting | bytes 2097152
  73.6 0.6 copy.11

commit v8 on v7

--- a/solution.py
+++ b/solution.py
@@ -226,7 +226,6 @@
     pair_product.wait_recv()
     keep(0, dot3(products[1], products[0], NN).T)
     offset[body] = constants[1, body] - dot3(constants[0, body], products[1], NT)
-    keep(1, products[0].T)
 
     @pl.when(chip == 0)
     def _():
@@ -322,6 +321,7 @@
         @pl.when(i == fix_turn)
         def _():
             pair_coupling.wait_recv()
+            keep(1, products[0].T)
             keep(2, square(couplings.at[0]))
             keep(3, square(couplings.at[1]))
 

time: 74.8 us -> 74.6 us (level)
  no operation moved by 1% of the time
where the time goes in v8:
time: 74.6 us; the launch traced here: 74.2 us
  Pallas kernels  71.9 us (96%)
  local copies, waits for them, and re-layouts  1.59 us (2%)
    pallas_call x1, Pallas kernels, on_device(): pl.pallas_call(functools.partial(kernel, panels, rows), out_shape=(jax.Sh...  71.9 us
    unnamed x2, local copies, waits for them, and re-layouts  1.59 us

profile of v8, /device:TPU:57, one launch (start us, length us, event | category | flops | bytes accessed | tf_op | source)
XLA Modules:
  0.0 74.2 jit_solution(4963823775315788622)
XLA Ops:
  0.6 71.9 %shard_map.77 = (f32[1024,256]{1,0:T(8,128)S(1)}, f32[32,256]{1,0:T(8,128)S(1)}) custom-call(f32[1024,256]{1,0:T(8,128)} %slab.1, f32[1024,256]{1,0:T(8,128)} %boundary.1, f32[16,256]{1,0:T(8,128)} %inverse_ref.1, f32[16,256]{1,0:T(8,128)} %beneath_ref.1, f32[16,256]{1,0:T(8,128)} %coupling_ref.1, f32[32,256]{1,0:T(8,128)} %cols_ref.1), custom_call_target="tpu_custom_call" | custom-call | tf_op jit(solution)/shard_map/pallas_call | solution.py:577
  72.6 1.0 %copy.10 = f32[1024,256]{1,0:T(8,128)} copy(f32[1024,256]{1,0:T(8,128)S(1)} %get-tuple-element.4) | data formatting | bytes 2097152
  73.5 0.6 copy.11
